TPU v7x, 512 devices: a whole 4x8x8 slice. The times are simulated.
512 devices in a mesh: section: 4 (over x), expert: 64 (over z, y), pair: 2 (over core).
Axes of the slice: x: 4, y: 8, z: 8, core: 2. Of those that a mesh axis runs over, the one named last changes fastest.
Arguments:
- initial_state: bfloat16 [32768, 2048], P(('section', 'expert')), may hold values from -6 to 6
- prelude: bfloat16 [32768, 2048], P(('section', 'expert')), may hold values from -6 to 6
- inject_gain: float32 [2048], replicated, may hold values from 0.1 to 1.9
- norm_gain: float32 [2048], replicated, may hold values from 0.1 to 1.9
- router: bfloat16 [2048, 64], replicated, may hold values from -0.125 to 0.125
- gate_w: bfloat16 [64, 2048, 1024], P('expert', 'section', 'pair'), may hold values from -0.125 to 0.125
- up_w: bfloat16 [64, 2048, 1024], P('expert', 'section', 'pair'), may hold values from -0.125 to 0.125
- down_w: bfloat16 [64, 1024, 2048], P('expert', 'pair', 'section'), may hold values from -0.1875 to 0.1875
- routes: int32 [1, 32768, 8], P(None, ('section', 'expert')), may hold values from 0 to 63, all different within a row; in each aligned block of 128 rows (0 to 127, 128 to 255, ..., all dimensions but the last counted through in order) at most 18 rows name the same one
Outputs:
- final_state: bfloat16 [32768, 2048], P(('section', 'expert'), 'pair')
Inputs may be any that keep to these rules, and one draw needn't show every extreme that they name: `routes`: each row names 8 different experts. Within the 128 rows of one device in one pass (aligned blocks of the token dimension), no expert is named more than 18 times, a bound that some block reaches.
All inputs are finite; a program needn't handle non-finite values.
Results may differ from a plain program's by a relative error of at most 0.0029.
Values may be sent and summed in bfloat16 or wider, within the bound.
No kernel may reach another device: no remote copies, remote signals or barrier semaphores. Data moves between devices by JAX's collectives and lax.ppermute only.
A program may use at most 64 MiB of HBM per device.

v0:
```python
import jax
import jax.numpy as jnp
from jax import lax
from jax.sharding import PartitionSpec as P

TOPK = 8
CAP = 18


def rows_first(arrays, axis, dims):
    turned = [jnp.moveaxis(a, dim, 0) for a, dim in zip(arrays, dims)]
    both = jnp.concatenate([t.reshape(len(t), -1) for t in turned], axis=1)
    out, at, done = (lax.all_gather(both, axis, axis=0, tiled=True), 0, [])
    for t, dim in zip(turned, dims):
        piece = out[:, at : at + t[0].size].reshape(-1, *t.shape[1:])
        done.append(jnp.moveaxis(piece, 0, dim))
        at += t[0].size
    return tuple(done)


def on_device(initial_state, prelude, inject_gain, norm_gain, router, gate_w, up_w, down_w, routes):
    gate_full, up_full, down_full = rows_first((gate_w, up_w, down_w), "section", (1, 1, 2))
    paired_w = jnp.concatenate([gate_full, up_full], axis=2)
    local_count = gate_full.shape[0]
    half_width = gate_full.shape[2]
    tok_count, model_width = initial_state.shape
    experts_all = router.shape[1]
    pair_count = lax.axis_size("pair")
    pair_pos = lax.axis_index("pair")
    part_width = model_width // pair_count
    hidden_state = initial_state.astype(jnp.float32)
    prelude_f = prelude.astype(jnp.float32)
    token_ids = jnp.broadcast_to(
        jnp.arange(tok_count, dtype=jnp.int32)[:, None], (tok_count, TOPK)
    ).reshape(-1)
    expert_range = jnp.arange(experts_all, dtype=jnp.int32)
    mixed_state = hidden_state + prelude_f * inject_gain
    inv_rms = lax.rsqrt(jnp.mean(mixed_state * mixed_state, axis=-1, keepdims=True) + 1e-06)
    normed = (mixed_state * inv_rms * norm_gain).astype(jnp.bfloat16)
    logits = jnp.dot(normed, router, preferred_element_type=jnp.float32)
    router_prob = jax.nn.sigmoid(logits)
    chosen = routes[0]
    onehot_k = (chosen[:, :, None] == expert_range).astype(jnp.float32)
    picked = jnp.sum(onehot_k * router_prob[:, None, :], axis=-1)
    gate_vals = picked / jnp.sum(picked, axis=1, keepdims=True)
    flat_ids = chosen.reshape(-1)
    onehot = (flat_ids[:, None] == expert_range).astype(jnp.int32)
    before = jnp.cumsum(onehot, axis=0) - onehot
    slot_rank = jnp.sum(before * onehot, axis=-1)
    slot_ids = flat_ids * CAP + slot_rank
    source_rows = jnp.full((experts_all * CAP,), tok_count, jnp.int32).at[slot_ids].set(token_ids)
    padded_rows = jnp.concatenate([normed, jnp.zeros((1, model_width), jnp.bfloat16)], axis=0)
    sender_rows = lax.dynamic_slice_in_dim(padded_rows, pair_pos * part_width, part_width, 1)
    outgoing = sender_rows[source_rows].reshape(experts_all, CAP, sender_rows.shape[1])
    received = lax.all_to_all(outgoing, "expert", split_axis=0, concat_axis=0, tiled=True)
    received = lax.all_gather(received, "pair", axis=2, tiled=True)
    slot_count = received.shape[1]
    grouped = received.reshape(-1, local_count, slot_count, model_width)
    gate_up = jnp.einsum("sekd,edh->sekh", grouped, paired_w, preferred_element_type=jnp.float32)
    inner_act = (jax.nn.silu(gate_up[..., :half_width]) * gate_up[..., half_width:]).astype(
        jnp.bfloat16
    )
    partial_out = jnp.einsum(
        "sekh,ehd->sekd", inner_act, down_full, preferred_element_type=jnp.float32
    ).astype(jnp.bfloat16)
    lead = partial_out.shape[0]
    pieces = jnp.moveaxis(
        partial_out.reshape(lead, local_count, slot_count, pair_count, part_width), 3, 0
    )
    arrived = lax.all_to_all(pieces, "pair", split_axis=0, concat_axis=0, tiled=True)
    summed = jnp.sum(arrived.astype(jnp.float32), axis=0).astype(jnp.bfloat16)
    returned_rows = lax.all_to_all(
        summed.reshape(-1, slot_count, summed.shape[-1]),
        "expert",
        split_axis=0,
        concat_axis=0,
        tiled=True,
    )
    back_width = returned_rows.shape[-1]
    flat_back = returned_rows.reshape(experts_all * CAP, back_width)
    taken_rows = flat_back[slot_ids].reshape(tok_count, TOPK, back_width)
    moe_out = jnp.sum(gate_vals[:, :, None] * taken_rows.astype(jnp.float32), axis=1)
    hidden_state = (
        lax.dynamic_slice_in_dim(mixed_state, pair_pos * part_width, part_width, 1) + moe_out
    )
    return hidden_state.astype(jnp.bfloat16)


def solution(mesh):
    placed = (
        P(("section", "expert"), None),
        P(("section", "expert"), None),
        P(),
        P(),
        P(),
        P("expert", "section", "pair"),
        P("expert", "section", "pair"),
        P("expert", "pair", "section"),
        P(None, ("section", "expert"), None),
    )
    return jax.shard_map(
        on_device,
        mesh=mesh,
        in_specs=placed,
        out_specs=P(("section", "expert"), "pair"),
        check_vma=False,
    )
```

profile of v0, /device:TPU:118, one launch (start us, length us, event | category | flops | bytes accessed | tf_op | source)
XLA Modules:
  0.0 317.9 jit_solution(2477167705918920072)
XLA Ops:
  6.5 1.3 copy.51
  7.9 2.5 pad_maximum_fusion
  10.4 0.1 copy.53
  11.1 18.0 %reduce-window.6 = s32[64,8,128]{2,1,0:T(8,128)S(1)} reduce-window(s32[64,8,128]{2,1,0:T(8,128)S(1)} %fusion.14, s32[]{:T(128)} %constant.13.clone.1), window={size=1x1x128 pad=0_0x0_0x127_0}, to_apply=%region_3.0 | reduce-window | flops 8323072 | bytes 524292 | tf_op jit(solution)/shard_map/reduce-window
  29.1 0.1 slice.35
  29.2 0.1 copy.55
  29.5 0.1 broadcast_add_fusion
  29.7 4.3 %scatter_custom_fusion = s32[1152]{0:T(1024)S(1)} fusion(s32[1024]{0:T(1024)S(1)} %bitcast.78, s32[1024]{0:T(1024)S(1)} %reshape.145, s32[]{:T(128)} %constant.12.clone.1), kind=kCustom, calls=%fused_computation.42 | custom fusion | bytes 4612 | tf_op jit(solution)/shard_map/scatter | solution.py:51
  34.1 0.3 multiply_reduce_fusion
  34.4 1.0 copy-done.1
  35.4 0.2 multiply_convert_fusion
  35.6 0.8 copy-done.3
  36.4 5.0 %gather_fusion = bf16[1152,1024]{1,0:T(8,128)(2,1)} fusion(bf16[129,1024]{1,0:T(8,128)(2,1)S(1)} %pad_dynamic-slice_fusion, s32[2048]{0:T(1024)S(1)} %pad_clamp_fusion), kind=kCustom, calls=%fused_computation | custom fusion | bytes 4723200 | tf_op jit(solution)/shard_map/gather | solution.py:54
  41.4 2.7 reshape.120
  44.1 88.4 %all_to_all.15 = bf16[64,18,1024]{2,1,0:T(8,128)(2,1)S(1)} all-to-all(bf16[64,18,1024]{2,1,0:T(8,128)(2,1)S(1)} %reshape.120), channel_id=1, replica_groups=mesh['section'=4,'expert'=64,'pair'=2] {'expert'}, dimensions={0} | all-to-all | bytes 4718592 | tf_op jit(solution)/shard_map/all_to_all | solution.py:55
  132.5 2.8 copy.57
  135.4 3.8 %slice_bitcast_fusion.1 = (bf16[1,2048,512]{2,1,0:T(8,128)(2,1)S(1)}, bf16[1,2048,512]{2,1,0:T(8,128)(2,1)}) fusion(bf16[2048,1536]{1,0:T(8,128)(2,1)} %all-gather.3.cloned.1.call-done), kind=kLoop, calls=%fused_computation.15 | loop fusion | bytes 8388608 | tf_op jit(solution)/shard_map/transpose;reshape | solution.py:16
  139.2 20.5 %all-gather.5.cloned.1.call-done = bf16[64,18,2048]{2,0,1:T(8,128)(2,1)} async-done(((bf16[64,18,1024]{2,0,1:T(8,128)(2,1)}), bf16[64,18,2048]{2,0,1:T(8,128)(2,1)}) %all-gather.5.cloned.1.call-update) | async-done | bytes 4718608 | tf_op jit(solution)/shard_map/all_gather | solution.py:56
  159.7 7.8 %fusion.5 = f32[64,1,18,1024]{3,0,2,1:T(8,128)S(1)} fusion(bf16[64,18,2048]{2,0,1:T(8,128)(2,1)} %all-gather.5.cloned.1.call-done, bf16[1,2048,512]{2,1,0:T(8,128)(2,1)} %get-tuple-element.10, bf16[1,2048,512]{2,1,0:T(8,128)(2,1)S(1)} %get-tuple-element.9), kind=kOutput, calls=%fused_computation.13 | convolution fusion | flops 4840226816 | bytes 13631488 | tf_op jit(solution)/shard_map/sekd,edh->sekh/dot_general | solution.py:59
  167.5 4.6 %convolution_convert_fusion = bf16[2048,64,18]{0,1,2:T(8,128)(2,1)S(1)} fusion(bf16[2048,1536]{1,0:T(8,128)(2,1)} %all-gather.3.cloned.1.call-done, f32[64,1,18,1024]{3,0,2,1:T(8,128)S(1)} %fusion.5), kind=kOutput, calls=%fused_computation.10 | convolution fusion | flops 2421817344 | bytes 11534336 | tf_op jit(solution)/shard_map/sekh,ehd->sekd/dot_general | solution.py:63
  172.1 0.7 copy.69
  172.8 8.6 %all_to_all.16 = bf16[2,64,1,18,1024]{4,1,3,2,0:T(8,128)(2,1)} all-to-all(bf16[2,64,1,18,1024]{4,1,3,2,0:T(8,128)(2,1)S(1)} %bitcast.69), channel_id=1, replica_groups=mesh['section'=4,'expert'=64,'pair'=2] {'pair'}, dimensions={0} | all-to-all | bytes 9437184 | tf_op jit(solution)/shard_map/all_to_all | solution.py:70
  181.4 4.0 %reduce_sum.64 = bf16[64,18,1024]{2,0,1:T(8,128)(2,1)S(1)} reduce(bf16[2,64,1,18,1024]{4,1,3,2,0:T(8,128)(2,1)} %all_to_all.16, bf16[]{:T(256)} %constant.11.clone.1), dimensions={0,2}, to_apply=%region_7.8 | reduce | flops 1179648 | bytes 7077890 | tf_op jit(solution)/shard_map/reduce_sum | solution.py:71
  185.4 3.1 copy.61
  188.5 13.4 %all-to-all-start.2 = ((bf16[64,18,1024]{2,1,0:T(8,128)(2,1)}), bf16[64,18,1024]{2,1,0:T(8,128)(2,1)}, u32[]{:S(2)}, u32[]{:S(2)}) async-start(bf16[64,18,1024]{2,1,0:T(8,128)(2,1)} %copy.61), calls=%async_computation.2 | async-start | bytes 6291456 | tf_op jit(solution)/shard_map/all_to_all | solution.py:72
  201.9 0.3 fusion.10
  202.3 0.1 copy.50
  202.4 96.5 %all-to-all-done.2 = bf16[64,18,1024]{2,1,0:T(8,128)(2,1)} async-done(((bf16[64,18,1024]{2,1,0:T(8,128)(2,1)}), bf16[64,18,1024]{2,1,0:T(8,128)(2,1)}, u32[]{:S(2)}, u32[]{:S(2)}) %all-to-all-start.2) | async-done | bytes 2359328 | tf_op jit(solution)/shard_map/all_to_all | solution.py:72
  298.9 2.9 reshape.123
  301.9 5.4 %gather_fusion.1 = bf16[1024,1024]{1,0:T(8,128)(2,1)} fusion(bf16[1152,1024]{1,0:T(8,128)(2,1)S(1)} %reshape.123, s32[1024]{0:T(1024)S(1)} %broadcast_clamp_fusion), kind=kCustom, calls=%fused_computation.1 | custom fusion | bytes 4198400 | tf_op jit(solution)/shard_map/gather | solution.py:81
  307.3 3.0 fusion.3
  310.3 0.8 add_convert_fusion
  (43 shorter events, 1.0 us)
Async XLA Ops:
  6.5 195.4 %copy-start = (bf16[2048,64]{0,1:T(8,128)(2,1)S(1)}, bf16[2048,64]{0,1:T(8,128)(2,1)}, u32[]{:S(2)}) copy-start(bf16[2048,64]{0,1:T(8,128)(2,1)} %param.13) | copy-start | bytes 786436
  6.5 128.8 %all-gather.3.cloned.1.call-start = ((), (), s32[]{:S(2)}) async-start(), calls=%async_computation.3 | async-start | bytes 7864320 | tf_op jit(solution)/shard_map/all_gather | solution.py:13
  7.8 2.6 copy-start.7
  10.3 23.7 %copy-start.5 = (bf16[128,2048]{1,0:T(8,128)(2,1)S(1)}, bf16[128,2048]{1,0:T(8,128)(2,1)}, u32[]{:S(2)}) copy-start(bf16[128,2048]{1,0:T(8,128)(2,1)} %param.10) | copy-start | bytes 1572868
  10.3 23.8 %copy-start.6 = (bf16[128,2048]{1,0:T(8,128)(2,1)S(1)}, bf16[128,2048]{1,0:T(8,128)(2,1)}, u32[]{:S(2)}) copy-start(bf16[128,2048]{1,0:T(8,128)(2,1)} %param.9) | copy-start | bytes 1572868
  10.3 23.8 %copy-start.8 = (f32[2048]{0:T(1024)S(1)}, f32[2048]{0:T(1024)}, u32[]{:S(2)}) copy-start(f32[2048]{0:T(1024)} %param.11) | copy-start | bytes 24580
  10.3 149.3 %all-gather.5.cloned.1.call-start = ((), (), s32[]{:S(2)}) async-start(), calls=%async_computation.4 | async-start | bytes 7077888 | tf_op jit(solution)/shard_map/all_gather | solution.py:56
  10.9 24.5 %copy-start.9 = (f32[2048]{0:T(1024)S(1)}, f32[2048]{0:T(1024)}, u32[]{:S(2)}) copy-start(f32[2048]{0:T(1024)} %param.12) | copy-start | bytes 24580
  34.4 1.0 copy-start.1
  35.6 0.8 copy-start.3
  188.5 13.4 %copy-start.4 = (bf16[128,2048]{1,0:T(8,128)(2,1)S(1)}, bf16[128,2048]{1,0:T(8,128)(2,1)}, u32[]{:S(2)}) copy-start(bf16[128,2048]{1,0:T(8,128)(2,1)} %copy-done.3) | copy-start | bytes 1572868
  188.5 110.4 %all-to-all-start.2 = ((bf16[64,18,1024]{2,1,0:T(8,128)(2,1)}), bf16[64,18,1024]{2,1,0:T(8,128)(2,1)}, u32[]{:S(2)}, u32[]{:S(2)}) async-start(bf16[64,18,1024]{2,1,0:T(8,128)(2,1)} %copy.61), calls=%async_computation.2 | async-start | bytes 6291456 | tf_op jit(solution)/shard_map/all_to_all | solution.py:72
  307.3 3.0 copy-start.2
Sparse Core Ops, SparseCore 0:
  10.5 73.0 all-gather.2
  135.5 24.1 all-gather.4
where the time goes:
time: 318 us
  waiting for transfers between devices  117 us (37%)
  blocking collectives  97 us (31%)
  local copies, waits for them, and re-layouts  34.9 us (11%)
  other arithmetic  29.1 us (9%)
  between operations  13.7 us (4%)
  starting transfers between devices  13.4 us (4%)
  matrix products  12.7 us (4%)
    all_to_all x1, waiting for transfers between devices, on_device(): lax.all_to_all(summed.reshape(-1, slot_count, summed.shape[-1]), 'expert'...  96.5 us
    all_to_all x1, blocking collectives, on_device(): lax.all_to_all(outgoing, 'expert', split_axis=0, concat_axis=0, tiled=True)  88.4 us
    all_gather x1, waiting for transfers between devices, on_device(): received = lax.all_gather(received, 'pair', axis=2, tiled=True)  20.5 us
    another operation x3, other arithmetic  18.2 us
    all_to_all x1, starting transfers between devices, on_device(): lax.all_to_all(summed.reshape(-1, slot_count, summed.shape[-1]), 'expert'...  13.4 us
    all_to_all x1, blocking collectives, on_device(): lax.all_to_all(pieces, 'pair', split_axis=0, concat_axis=0, tiled=True)  8.61 us
    dot_general x1, matrix products, on_device(): jnp.einsum('sekd,edh->sekh', grouped, paired_w, preferred_element_type=jn...  7.82 us
  transfers between devices with their start and end apart: 3, of which 2 were waited for; matrix products, arithmetic and copies ran while one was open for 12% of the time, Pallas kernels for 0%

commit v1 on v0

v1 whole, which is shorter than its diff:
```python
import jax
import jax.numpy as jnp
from jax import lax
from jax.experimental import pallas as pl
from jax.experimental.pallas import tpu as pltpu
from jax.sharding import PartitionSpec as P


TOPK = 8
CAP = 18
MAIN = 8
HALF_CAP = CAP // 2
LANES = 128
F32 = jnp.float32
BF16 = jnp.bfloat16
VMEM = pl.BlockSpec(memory_space=pltpu.VMEM)
SMEM = pl.BlockSpec(memory_space=pltpu.SMEM)
FAR = pl.BlockSpec(memory_space=pltpu.HBM)


def dot(a, b):
    return jnp.dot(a, b, preferred_element_type=F32)


def dot_t(a, b):
    return lax.dot_general(a, b, (((0,), (0,)), ((), ())), preferred_element_type=F32)


def route_kernel(where_ref, *refs):
    stored, refs = refs[:6], refs[6:]
    send_ref, main_hi_ref, main_lo_ref, last_hi_ref, last_lo_ref = refs[:5]
    held, sems = refs[5:11], refs[11]
    copies = [pltpu.make_async_copy(stored[i], held[i], sems.at[i]) for i in range(6)]
    for copy in copies:
        copy.start()
    for copy in copies:
        copy.wait()
    state_ref, prelude_ref, inject_ref, gain_ref, router_ref, routes_ref = held
    tokens, width = state_ref.shape
    experts = router_ref.shape[0]
    blocks = width // LANES
    low = where_ref[0] * HALF_CAP
    mixed = state_ref[...].astype(F32) + prelude_ref[...].astype(F32) * inject_ref[...]
    inv_rms = lax.rsqrt(jnp.mean(mixed * mixed, axis=-1, keepdims=True) + 1e-06)
    normed = (mixed * inv_rms * gain_ref[...]).astype(BF16)
    logits = lax.dot_general(
        normed, router_ref[...], (((1,), (1,)), ((), ())), preferred_element_type=F32
    )
    prob = jax.nn.sigmoid(logits)
    routes = routes_ref[...].astype(F32).T.astype(jnp.int32)
    expert = lax.broadcasted_iota(jnp.int32, (tokens, experts), 1)
    chosen = routes[:, 0:1] == expert
    for k in range(1, TOPK):
        chosen = jnp.logical_or(chosen, routes[:, k : k + 1] == expert)
    chosen_f = chosen.astype(F32)
    earlier = lax.broadcasted_iota(jnp.int32, (tokens, tokens), 1) < lax.broadcasted_iota(
        jnp.int32, (tokens, tokens), 0
    )
    rank = dot(earlier.astype(F32).astype(BF16), chosen_f.astype(BF16))
    place = jnp.where(chosen, rank + 1.0, 0.0)
    picked = chosen_f * prob
    gate = picked / jnp.sum(picked, axis=1, keepdims=True)
    gate_hi = gate.astype(BF16)
    gate_lo = (gate - gate_hi.astype(F32)).astype(BF16)
    lane = lax.broadcasted_iota(jnp.int32, (experts, experts * MAIN), 1)
    row = lax.broadcasted_iota(jnp.int32, (experts, experts * MAIN), 0)
    spread = (lane // MAIN == row).astype(F32).astype(BF16)
    slot = lax.broadcasted_iota(jnp.int32, (tokens, experts * MAIN), 1) % MAIN + (1 + low)
    at_main = dot(place.astype(BF16), spread) == slot.astype(F32)
    at_last = place == (low + HALF_CAP).astype(F32)
    main_hi_ref[...] = jnp.where(at_main, dot(gate_hi, spread), 0.0).astype(BF16)
    main_lo_ref[...] = jnp.where(at_main, dot(gate_lo, spread), 0.0).astype(BF16)
    last_hi_ref[...] = jnp.where(at_last, gate_hi.astype(F32), 0.0).astype(BF16)
    last_lo_ref[...] = jnp.where(at_last, gate_lo.astype(F32), 0.0).astype(BF16)
    pick_main = at_main.astype(F32).astype(BF16)
    pick_last = at_last.astype(F32).astype(BF16)
    for pair in range(blocks // 2):
        cols = normed[:, pair * 2 * LANES : (pair + 1) * 2 * LANES]
        rows = dot_t(pick_main, cols)
        for j in range(2):
            c = 2 * pair + j
            send_ref[:, c * MAIN : (c + 1) * MAIN, :] = (
                rows[:, j * LANES : (j + 1) * LANES].reshape(experts, MAIN, LANES).astype(BF16)
            )
    last = dot_t(pick_last, normed)
    send_ref[:, blocks * MAIN :, :] = last.reshape(experts, blocks, LANES).astype(BF16)


def ffn_kernel(where_ref, rows_ref, *refs):
    stored, back_ref, x_ref, act_ref = refs[:10], refs[10], refs[11], refs[12]
    weights, sems = refs[13:23], refs[23]
    sections, _, part = x_ref.shape
    experts = rows_ref.shape[0]
    blocks = sections * part // LANES
    per = part // LANES
    main = experts * MAIN
    here = where_ref[1]
    step = 256
    copies = [
        pltpu.make_async_copy(stored[i], weights[i], sems.at[i]) for i in range(len(stored))
    ]
    for copy in copies:
        copy.start()
    last = rows_ref[:, blocks * MAIN :, :].astype(F32).reshape(experts, blocks * LANES)
    for s in range(sections):
        for c in range(per):
            b = s * per + c
            x_ref[s, :main, c * LANES : (c + 1) * LANES] = (
                rows_ref[:, b * MAIN : (b + 1) * MAIN, :].reshape(main, LANES)
            )
        x_ref[s, main:, :] = last[:, s * part : (s + 1) * part].astype(BF16)
    offsets = (0, 1, 3, 2)
    at = [lax.rem(here + d, sections) for d in offsets]

    def piece(q, d, first, size, cols):
        own = weights[q * 5 : q * 5 + 5]
        if offsets[d] != 2:
            return own[d][first : first + size, cols]
        edge = own[3].shape[0]
        if first + size <= edge:
            return own[3][first : first + size, cols]
        return own[4][first - edge : first - edge + size, cols]

    for q in range(2):
        for copy in copies[q * 5 : q * 5 + 5]:
            copy.wait()
        for n in range(part // step):
            cols = slice(n * step, (n + 1) * step)
            total = [None, None]
            for which in range(2):
                for d in range(sections):
                    for k in range(part // step):
                        term = dot(
                            x_ref[at[d], :, k * step : (k + 1) * step],
                            piece(q, d, which * part + k * step, step, cols),
                        )
                        total[which] = term if total[which] is None else total[which] + term
            act = jax.nn.silu(total[0]) * total[1]
            act_ref[:, q * part + n * step : q * part + (n + 1) * step] = act.astype(BF16)
    for d in range(sections):
        wide = []
        for n in range(part // step):
            cols = slice(n * step, (n + 1) * step)
            total = None
            for q in range(2):
                partial = None
                for k in range(part // step):
                    term = dot(
                        act_ref[:, q * part + k * step : q * part + (k + 1) * step],
                        piece(q, d, 2 * part + k * step, step, cols),
                    )
                    partial = term if partial is None else partial + term
                partial = partial.astype(BF16).astype(F32)
                total = partial if total is None else total + partial
            for j in range(step // LANES):
                b = at[d] * per + n * (step // LANES) + j
                back_ref[:, pl.ds(pl.multiple_of(b * MAIN, MAIN), MAIN), :] = (
                    total[:main, j * LANES : (j + 1) * LANES]
                    .reshape(experts, MAIN, LANES)
                    .astype(BF16)
                )
            wide.append(total[main:])
        x_ref[at[d], main:, :] = jnp.concatenate(wide, axis=1).astype(BF16)
    whole = jnp.concatenate([x_ref[s, main:, :] for s in range(sections)], axis=1)
    back_ref[:, blocks * MAIN :, :] = (
        whole.astype(F32).reshape(experts, blocks, LANES).astype(BF16)
    )


def combine_half(half, rows_ref, main_hi, main_lo, last_hi, last_lo):
    experts = rows_ref.shape[0]
    blocks = rows_ref.shape[1] // HALF_CAP
    mine = blocks // 2
    main = experts * MAIN
    outs = []
    for pair in range(mine // 2):
        cols = []
        for j in range(2):
            b = half * mine + pair * 2 + j
            cols.append(
                rows_ref[:, pl.ds(pl.multiple_of(b * MAIN, MAIN), MAIN), :].reshape(main, LANES)
            )
        rows = jnp.concatenate(cols, axis=1)
        outs.append(dot(main_hi, rows) + dot(main_lo, rows))
    total = jnp.concatenate(outs, axis=1)
    first = pl.multiple_of(blocks * MAIN + half * mine, MAIN)
    last = rows_ref[:, pl.ds(first, mine), :].astype(F32)
    last = last.reshape(experts, mine * LANES).astype(BF16)
    return total + dot(last_hi, last) + dot(last_lo, last)


def send_half_kernel(where_ref, rows_ref, mh_ref, ml_ref, lh_ref, ll_ref, out_ref):
    out_ref[...] = combine_half(
        1 - where_ref[0], rows_ref, mh_ref[...], ml_ref[...], lh_ref[...], ll_ref[...]
    ).astype(BF16)


def keep_half_kernel(
    where_ref, rows_ref, mh_ref, ml_ref, lh_ref, ll_ref, state_ref, prelude_ref, inject_ref, out_ref
):
    width = out_ref.shape[1]
    half = where_ref[0]
    moe = combine_half(half, rows_ref, mh_ref[...], ml_ref[...], lh_ref[...], ll_ref[...])
    cols = pl.ds(pl.multiple_of(half * width, width), width)
    mixed = state_ref[:, cols].astype(F32) + prelude_ref[:, cols].astype(F32) * inject_ref[:, cols]
    out_ref[...] = mixed + moe


def call(kernel, outs, n_in, scratch=(), limit=10, cost=None, far=0):
    return pl.pallas_call(
        kernel,
        out_shape=outs,
        in_specs=[SMEM] + [VMEM] * (n_in - 1 - far) + [FAR] * far,
        out_specs=jax.tree.map(lambda _: VMEM, outs),
        scratch_shapes=list(scratch),
        cost_estimate=cost,
        compiler_params=pltpu.CompilerParams(vmem_limit_bytes=limit << 20),
    )


def one_pass(initial_state, prelude, inject_gain, norm_gain, router, gate_w, up_w, down_w, routes):
    tokens, width = initial_state.shape
    experts = router.shape[1]
    blocks = width // LANES
    sections = lax.axis_size("section")
    part = gate_w.shape[1]
    where = jnp.stack([lax.axis_index("pair"), lax.axis_index("section")]).astype(jnp.int32)
    inject = inject_gain[None, :]
    shape = jax.ShapeDtypeStruct

    up_ring = [(i, (i + 1) % sections) for i in range(sections)]
    down_ring = [(i, (i - 1) % sections) for i in range(sections)]
    swap = [(0, 1), (1, 0)]
    own = jnp.concatenate([gate_w[0], up_w[0], down_w[0]], axis=0)
    before = lax.ppermute(own, "section", up_ring)
    after = lax.ppermute(own, "section", down_ring)
    cut = own.shape[0] // 2
    far_a = lax.ppermute(before[:cut], "section", up_ring)
    far_b = lax.ppermute(after[cut:], "section", down_ring)
    mine = [own, after, before, far_a, far_b]
    other = [lax.ppermute(w, "pair", swap) for w in mine]

    message = shape((experts, blocks * HALF_CAP, LANES), BF16)
    send, main_hi, main_lo, last_hi, last_lo = call(
        route_kernel,
        (message,) + (shape((tokens, experts * MAIN), BF16),) * 2 + (shape((tokens, experts), BF16),) * 2,
        7,
        scratch=[
            pltpu.VMEM((tokens, width), BF16),
            pltpu.VMEM((tokens, width), BF16),
            pltpu.VMEM((1, width), F32),
            pltpu.VMEM((1, width), F32),
            pltpu.VMEM((experts, width), BF16),
            pltpu.VMEM((TOPK, tokens), jnp.int32),
            pltpu.SemaphoreType.DMA((6,)),
        ],
        limit=60,
        far=6,
    )(where, initial_state, prelude, inject, norm_gain[None, :], router.T, routes[0].T)
    received = lax.all_to_all(send, "expert", split_axis=0, concat_axis=0, tiled=True)
    back = call(
        ffn_kernel,
        message,
        12,
        scratch=[
            pltpu.VMEM((sections, experts * HALF_CAP, part), BF16),
            pltpu.VMEM((experts * HALF_CAP, 2 * part), BF16),
            *[pltpu.VMEM(w.shape, BF16) for w in mine + other],
            pltpu.SemaphoreType.DMA((len(mine + other),)),
        ],
        limit=60,
        far=len(mine + other),
    )(where, received, *mine, *other)
    returned = lax.all_to_all(back, "expert", split_axis=0, concat_axis=0, tiled=True)
    weights = (main_hi, main_lo, last_hi, last_lo)
    half = width // 2
    given = call(send_half_kernel, shape((tokens, half), BF16), 6)(where, returned, *weights)
    got = lax.ppermute(given, "pair", swap)
    kept = call(keep_half_kernel, shape((tokens, half), F32), 9)(
        where, returned, *weights, initial_state, prelude, inject
    )
    return (kept + got.astype(F32)).astype(BF16)


def solution(mesh):
    placed = (
        P(("section", "expert"), None),
        P(("section", "expert"), None),
        P(),
        P(),
        P(),
        P("expert", "section", "pair"),
        P("expert", "section", "pair"),
        P("expert", "pair", "section"),
        P(None, ("section", "expert"), None),
    )
    return jax.shard_map(
        one_pass,
        mesh=mesh,
        in_specs=placed,
        out_specs=P(("section", "expert"), "pair"),
        check_vma=False,
    )
```

time: 318 us -> 187 us (0.59)
  the two profiles are of different devices: /device:TPU:118 before, /device:TPU:1 now
where the time goes in v1:
time: 187 us
  blocking collectives  71 us (38%)
  starting transfers between devices  50 us (27%)
  waiting for transfers between devices  38 us (20%)
  Pallas kernels  21.2 us (11%)
  local copies, waits for them, and re-layouts  3.64 us (2%)
  other arithmetic  2.5 us (1%)
    all_to_all x1, blocking collectives, one_pass(): lax.all_to_all(back, 'expert', split_axis=0, concat_axis=0, tiled=True)  71 us
    ppermute x1, waiting for transfers between devices, one_pass(): before = lax.ppermute(own, 'section', up_ring)  28.2 us
    all_to_all x1, starting transfers between devices, one_pass(): lax.all_to_all(send, 'expert', split_axis=0, concat_axis=0, tiled=True)  17.3 us
    ppermute x5, starting transfers between devices, one_pass(): other = [lax.ppermute(w, 'pair', swap) for w in mine]  16.1 us
    pallas_call x1, Pallas kernels, one_pass(): call(ffn_kernel, message, 12, scratch=[pltpu.VMEM((sections, experts * HA...  13.8 us
    ppermute x1, waiting for transfers between devices, one_pass(): far_a = lax.ppermute(before[:cut], 'section', up_ring)  7.57 us
    pallas_call x1, Pallas kernels, one_pass(): call(route_kernel, (message,) + (shape((tokens, experts * MAIN), BF16),)...  5.19 us
    ppermute x1, starting transfers between devices, one_pass(): far_b = lax.ppermute(after[cut:], 'section', down_ring)  4.57 us
  transfers between devices with their start and end apart: 11, of which 3 were waited for; matrix products, arithmetic and copies ran while one was open for 1% of the time, Pallas kernels for 1%

profile of v1, /device:TPU:1, one launch (start us, length us, event | category | flops | bytes accessed | tf_op | source)
XLA Modules:
  0.0 186.7 jit_solution(16995072522206890225)
XLA Ops:
  0.0 0.6 pad_add_fusion.where_ref
  0.6 5.2 %shard_map.91 = (bf16[64,144,128]{2,1,0:T(8,128)(2,1)}, bf16[128,512]{1,0:T(8,128)(2,1)}, bf16[128,512]{1,0:T(8,128)(2,1)}, bf16[128,64]{1,0:T(8,128)(2,1)}, bf16[128,64]{1,0:T(8,128)(2,1)}) custom-call(s32[2]{0:T(128)} %pad_add_fusion.where_ref, bf16[128,2048]{1,0:T(8,128)(2,1)} %state_ref.1, bf16[128,2048]{1,0:T(8,128)(2,1)} %prelude_ref.1, ...), custom_call_target="tpu_custom_call" | custom-call | tf_op jit(solution)/shard_map/pallas_call | solution.py:244
  5.8 0.0 copy-start.18
  5.8 0.0 copy-start.19
  5.8 17.3 %all-to-all-start = ((bf16[64,144,128]{2,1,0:T(8,128)(2,1)}), bf16[64,144,128]{2,1,0:T(8,128)(2,1)S(1)}, u32[]{:S(2)}, u32[]{:S(2)}) async-start(bf16[64,144,128]{2,1,0:T(8,128)(2,1)} %get-tuple-element.10), calls=%async_computation | async-start | bytes 4718592 | tf_op jit(solution)/shard_map/all_to_all | solution.py:260
  23.1 1.1 pad_maximum_fusion.refs_0_
  24.3 3.1 %collective-permute-start.1 = (bf16[1536,512]{1,0:T(8,128)(2,1)S(1)}, bf16[1536,512]{1,0:T(8,128)(2,1)S(1)}, u32[]{:S(2)}, u32[]{:S(2)}) collective-permute-start(bf16[1536,512]{1,0:T(8,128)(2,1)S(1)} %pad_maximum_fusion.refs_0_), channel_id=1, source_target_pairs={{0,128},{128,256},{256,384},{384,0},{1,129},{129,257},{257,385},{3... | collective-permute-start | bytes 4718600 | tf_op jit(solution)/shard_map/ppermute | solution.py:235
  27.4 3.4 %collective-permute-start = (bf16[1536,512]{1,0:T(8,128)(2,1)S(1)}, bf16[1536,512]{1,0:T(8,128)(2,1)S(1)}, u32[]{:S(2)}, u32[]{:S(2)}) collective-permute-start(bf16[1536,512]{1,0:T(8,128)(2,1)S(1)} %pad_maximum_fusion.refs_0_), channel_id=1, source_target_pairs={{0,384},{128,0},{256,128},{384,256},{1,385},{129,1},{257,129},{385... | collective-permute-start | bytes 4718600 | tf_op jit(solution)/shard_map/ppermute | solution.py:236
  30.8 3.4 %collective-permute-start.4 = (bf16[1536,512]{1,0:T(8,128)(2,1)S(1)}, bf16[1536,512]{1,0:T(8,128)(2,1)S(1)}, u32[]{:S(2)}, u32[]{:S(2)}) collective-permute-start(bf16[1536,512]{1,0:T(8,128)(2,1)S(1)} %pad_maximum_fusion.refs_0_), channel_id=1, source_target_pairs={{0,1},{1,0},{2,3},{3,2},{4,5},{5,4},{6,7},{7,6},{8,9},{9,8},{10,11... | collective-permute-start | bytes 4718600 | tf_op jit(solution)/shard_map/ppermute | solution.py:241
  34.2 28.2 %collective-permute-done.1.refs_2_ = bf16[1536,512]{1,0:T(8,128)(2,1)S(1)} collective-permute-done((bf16[1536,512]{1,0:T(8,128)(2,1)S(1)}, bf16[1536,512]{1,0:T(8,128)(2,1)S(1)}, u32[]{:S(2)}, u32[]{:S(2)}) %collective-permute-start.1) | collective-permute-done | bytes 1572896 | tf_op jit(solution)/shard_map/ppermute | solution.py:235
  62.4 0.1 slice.8
  62.4 1.9 %collective-permute-start.2 = (bf16[768,512]{1,0:T(8,128)(2,1)S(1)}, bf16[768,512]{1,0:T(8,128)(2,1)S(1)}, u32[]{:S(2)}, u32[]{:S(2)}) collective-permute-start(bf16[768,512]{1,0:T(8,128)(2,1)S(1)} %slice.8), channel_id=1, source_target_pairs={{0,128},{128,256},{256,384},{384,0},{1,129},{129,257},{257,385},{3... | collective-permute-start | bytes 2359304 | tf_op jit(solution)/shard_map/ppermute | solution.py:238
  64.4 0.0 collective-permute-done.refs_1_
  64.4 0.1 slice.9
  64.5 4.6 %collective-permute-start.3 = (bf16[768,512]{1,0:T(8,128)(2,1)S(1)}, bf16[768,512]{1,0:T(8,128)(2,1)S(1)}, u32[]{:S(2)}, u32[]{:S(2)}) collective-permute-start(bf16[768,512]{1,0:T(8,128)(2,1)S(1)} %slice.9), channel_id=1, source_target_pairs={{0,384},{128,0},{256,128},{384,256},{1,385},{129,1},{257,129},{385... | collective-permute-start | bytes 2359304 | tf_op jit(solution)/shard_map/ppermute | solution.py:239
  69.0 4.3 %collective-permute-start.5 = (bf16[1536,512]{1,0:T(8,128)(2,1)S(1)}, bf16[1536,512]{1,0:T(8,128)(2,1)S(1)}, u32[]{:S(2)}, u32[]{:S(2)}) collective-permute-start(bf16[1536,512]{1,0:T(8,128)(2,1)S(1)} %collective-permute-done.refs_1_), channel_id=1, source_target_pairs={{0,1},{1,0},{2,3},{3,2},{4,5},{5,4},{6,7},{7,6},{8,9},{9,8},{10,11... | collective-permute-start | bytes 4718600 | tf_op jit(solution)/shard_map/ppermute | solution.py:241
  73.3 1.9 %collective-permute-start.6 = (bf16[1536,512]{1,0:T(8,128)(2,1)S(1)}, bf16[1536,512]{1,0:T(8,128)(2,1)}, u32[]{:S(2)}, u32[]{:S(2)}) collective-permute-start(bf16[1536,512]{1,0:T(8,128)(2,1)S(1)} %collective-permute-done.1.refs_2_), channel_id=1, source_target_pairs={{0,1},{1,0},{2,3},{3,2},{4,5},{5,4},{6,7},{7,6},{8,9},{9,8},{10,11... | collective-permute-start | bytes 4718600 | tf_op jit(solution)/shard_map/ppermute | solution.py:241
  75.3 7.6 %collective-permute-done.2.refs_3_ = bf16[768,512]{1,0:T(8,128)(2,1)S(1)} collective-permute-done((bf16[768,512]{1,0:T(8,128)(2,1)S(1)}, bf16[768,512]{1,0:T(8,128)(2,1)S(1)}, u32[]{:S(2)}, u32[]{:S(2)}) %collective-permute-start.2) | collective-permute-done | bytes 786464 | tf_op jit(solution)/shard_map/ppermute | solution.py:238
  82.8 4.6 %collective-permute-start.7 = (bf16[768,512]{1,0:T(8,128)(2,1)S(1)}, bf16[768,512]{1,0:T(8,128)(2,1)S(1)}, u32[]{:S(2)}, u32[]{:S(2)}) collective-permute-start(bf16[768,512]{1,0:T(8,128)(2,1)S(1)} %collective-permute-done.2.refs_3_), channel_id=1, source_target_pairs={{0,1},{1,0},{2,3},{3,2},{4,5},{5,4},{6,7},{7,6},{8,9},{9,8},{10,11... | collective-permute-start | bytes 2359304 | tf_op jit(solution)/shard_map/ppermute | solution.py:241
  87.4 1.9 %collective-permute-start.8 = (bf16[768,512]{1,0:T(8,128)(2,1)S(1)}, bf16[768,512]{1,0:T(8,128)(2,1)S(1)}, u32[]{:S(2)}, u32[]{:S(2)}) collective-permute-start(bf16[768,512]{1,0:T(8,128)(2,1)S(1)} %collective-permute-done.3.refs_4_), channel_id=1, source_target_pairs={{0,1},{1,0},{2,3},{3,2},{4,5},{5,4},{6,7},{7,6},{8,9},{9,8},{10,11... | collective-permute-start | bytes 2359304 | tf_op jit(solution)/shard_map/ppermute | solution.py:241
  89.4 0.0 collective-permute-done.4.refs_5_
  89.4 2.2 %collective-permute-done.8.refs_9_ = bf16[768,512]{1,0:T(8,128)(2,1)S(1)} collective-permute-done((bf16[768,512]{1,0:T(8,128)(2,1)S(1)}, bf16[768,512]{1,0:T(8,128)(2,1)S(1)}, u32[]{:S(2)}, u32[]{:S(2)}) %collective-permute-start.8) | collective-permute-done | bytes 786464 | tf_op jit(solution)/shard_map/ppermute | solution.py:241
  91.6 0.9 copy-done.17
  92.5 1.2 copy-done.13
  93.7 1.4 copy-done.8
  95.1 13.8 %shard_map.92 = bf16[64,144,128]{2,1,0:T(8,128)(2,1)} custom-call(s32[2]{0:T(128)} %pad_add_fusion.where_ref, bf16[64,144,128]{2,1,0:T(8,128)(2,1)} %copy-done.8, bf16[1536,512]{1,0:T(8,128)(2,1)} %copy-done.9, bf16[1536,512]{1,0:T(8,128)(2,1)} %copy-done.11, bf16[1536,512]{1,0:T(8,128)(2,1)} %copy-done.10, bf16[768,512]{1,0:T(8,128)(2,1)} %copy-done.14, ...), custom_call_target="tpu_custom_call" | custom-call | tf_op jit(solution)/shard_map/pallas_call | solution.py:261
  108.9 0.0 copy-start.2
  109.0 71.0 %all_to_all.10.rows_ref = bf16[64,144,128]{2,1,0:T(8,128)(2,1)S(1)} all-to-all(bf16[64,144,128]{2,1,0:T(8,128)(2,1)} %shard_map.92), channel_id=1, replica_groups=mesh['section'=4,'expert'=64,'pair'=2] {'expert'}, dimensions={0} | all-to-all | bytes 4718592 | tf_op jit(solution)/shard_map/all_to_all | solution.py:274
  180.0 1.1 shard_map.94
  181.1 3.7 %collective-permute-start.9 = (bf16[128,1024]{1,0:T(8,128)(2,1)S(1)}, bf16[128,1024]{1,0:T(8,128)(2,1)S(1)}, u32[]{:S(2)}, u32[]{:S(2)}) collective-permute-start(bf16[128,1024]{1,0:T(8,128)(2,1)S(1)} %shard_map.94), channel_id=1, source_target_pairs={{0,1},{1,0},{2,3},{3,2},{4,5},{5,4},{6,7},{7,6},{8,9},{9,8},{10,11... | collective-permute-start | bytes 786440 | tf_op jit(solution)/shard_map/ppermute | solution.py:278
  184.8 1.1 shard_map.93
  186.0 0.8 add_convert_fusion
  (40 shorter events, 0.1 us)
Async XLA Ops:
  5.8 17.3 %copy-start.18 = (bf16[1,512,512]{2,1,0:T(8,128)(2,1)S(1)}, bf16[1,512,512]{2,1,0:T(8,128)(2,1)}, u32[]{:S(2)}) copy-start(bf16[1,512,512]{2,1,0:T(8,128)(2,1)} %param.16) | copy-start | bytes 1572868
  5.8 17.3 %copy-start.19 = (bf16[1,512,512]{2,1,0:T(8,128)(2,1)S(1)}, bf16[1,512,512]{2,1,0:T(8,128)(2,1)}, u32[]{:S(2)}) copy-start(bf16[1,512,512]{2,1,0:T(8,128)(2,1)} %param.15) | copy-start | bytes 1572868
  5.8 87.9 %all-to-all-start = ((bf16[64,144,128]{2,1,0:T(8,128)(2,1)}), bf16[64,144,128]{2,1,0:T(8,128)(2,1)S(1)}, u32[]{:S(2)}, u32[]{:S(2)}) async-start(bf16[64,144,128]{2,1,0:T(8,128)(2,1)} %get-tuple-element.10), calls=%async_computation | async-start | bytes 4718592 | tf_op jit(solution)/shard_map/all_to_all | solution.py:260
  24.3 40.2 %copy-start.9 = (bf16[1536,512]{1,0:T(8,128)(2,1)}, bf16[1536,512]{1,0:T(8,128)(2,1)S(1)}, u32[]{:S(2)}) copy-start(bf16[1536,512]{1,0:T(8,128)(2,1)S(1)} %pad_maximum_fusion.refs_0_) | copy-start | bytes 4718596
  24.3 38.1 %collective-permute-start.1 = (bf16[1536,512]{1,0:T(8,128)(2,1)S(1)}, bf16[1536,512]{1,0:T(8,128)(2,1)S(1)}, u32[]{:S(2)}, u32[]{:S(2)}) collective-permute-start(bf16[1536,512]{1,0:T(8,128)(2,1)S(1)} %pad_maximum_fusion.refs_0_), channel_id=1, source_target_pairs={{0,128},{128,256},{256,384},{384,0},{1,129},{129,257},{257,385},{3... | collective-permute-start | bytes 4718600 | tf_op jit(solution)/shard_map/ppermute | solution.py:235
  27.4 37.0 %collective-permute-start = (bf16[1536,512]{1,0:T(8,128)(2,1)S(1)}, bf16[1536,512]{1,0:T(8,128)(2,1)S(1)}, u32[]{:S(2)}, u32[]{:S(2)}) collective-permute-start(bf16[1536,512]{1,0:T(8,128)(2,1)S(1)} %pad_maximum_fusion.refs_0_), channel_id=1, source_target_pairs={{0,384},{128,0},{256,128},{384,256},{1,385},{129,1},{257,129},{385... | collective-permute-start | bytes 4718600 | tf_op jit(solution)/shard_map/ppermute | solution.py:236
  30.8 58.6 %collective-permute-start.4 = (bf16[1536,512]{1,0:T(8,128)(2,1)S(1)}, bf16[1536,512]{1,0:T(8,128)(2,1)S(1)}, u32[]{:S(2)}, u32[]{:S(2)}) collective-permute-start(bf16[1536,512]{1,0:T(8,128)(2,1)S(1)} %pad_maximum_fusion.refs_0_), channel_id=1, source_target_pairs={{0,1},{1,0},{2,3},{3,2},{4,5},{5,4},{6,7},{7,6},{8,9},{9,8},{10,11... | collective-permute-start | bytes 4718600 | tf_op jit(solution)/shard_map/ppermute | solution.py:241
  62.4 10.9 %copy-start.10 = (bf16[1536,512]{1,0:T(8,128)(2,1)}, bf16[1536,512]{1,0:T(8,128)(2,1)S(1)}, u32[]{:S(2)}) copy-start(bf16[1536,512]{1,0:T(8,128)(2,1)S(1)} %collective-permute-done.1.refs_2_) | copy-start | bytes 4718596
  62.4 20.4 %collective-permute-start.2 = (bf16[768,512]{1,0:T(8,128)(2,1)S(1)}, bf16[768,512]{1,0:T(8,128)(2,1)S(1)}, u32[]{:S(2)}, u32[]{:S(2)}) collective-permute-start(bf16[768,512]{1,0:T(8,128)(2,1)S(1)} %slice.8), channel_id=1, source_target_pairs={{0,128},{128,256},{256,384},{384,0},{1,129},{129,257},{257,385},{3... | collective-permute-start | bytes 2359304 | tf_op jit(solution)/shard_map/ppermute | solution.py:238
  64.4 27.2 %copy-start.11 = (bf16[1536,512]{1,0:T(8,128)(2,1)}, bf16[1536,512]{1,0:T(8,128)(2,1)S(1)}, u32[]{:S(2)}) copy-start(bf16[1536,512]{1,0:T(8,128)(2,1)S(1)} %collective-permute-done.refs_1_) | copy-start | bytes 4718596
  64.5 23.0 %collective-permute-start.3 = (bf16[768,512]{1,0:T(8,128)(2,1)S(1)}, bf16[768,512]{1,0:T(8,128)(2,1)S(1)}, u32[]{:S(2)}, u32[]{:S(2)}) collective-permute-start(bf16[768,512]{1,0:T(8,128)(2,1)S(1)} %slice.9), channel_id=1, source_target_pairs={{0,384},{128,0},{256,128},{384,256},{1,385},{129,1},{257,129},{385... | collective-permute-start | bytes 2359304 | tf_op jit(solution)/shard_map/ppermute | solution.py:239
  69.0 22.6 %collective-permute-start.5 = (bf16[1536,512]{1,0:T(8,128)(2,1)S(1)}, bf16[1536,512]{1,0:T(8,128)(2,1)S(1)}, u32[]{:S(2)}, u32[]{:S(2)}) collective-permute-start(bf16[1536,512]{1,0:T(8,128)(2,1)S(1)} %collective-permute-done.refs_1_), channel_id=1, source_target_pairs={{0,1},{1,0},{2,3},{3,2},{4,5},{5,4},{6,7},{7,6},{8,9},{9,8},{10,11... | collective-permute-start | bytes 4718600 | tf_op jit(solution)/shard_map/ppermute | solution.py:241
  73.3 20.4 %collective-permute-start.6 = (bf16[1536,512]{1,0:T(8,128)(2,1)S(1)}, bf16[1536,512]{1,0:T(8,128)(2,1)}, u32[]{:S(2)}, u32[]{:S(2)}) collective-permute-start(bf16[1536,512]{1,0:T(8,128)(2,1)S(1)} %collective-permute-done.1.refs_2_), channel_id=1, source_target_pairs={{0,1},{1,0},{2,3},{3,2},{4,5},{5,4},{6,7},{7,6},{8,9},{9,8},{10,11... | collective-permute-start | bytes 4718600 | tf_op jit(solution)/shard_map/ppermute | solution.py:241
  82.8 10.9 %copy-start.14 = (bf16[768,512]{1,0:T(8,128)(2,1)}, bf16[768,512]{1,0:T(8,128)(2,1)S(1)}, u32[]{:S(2)}) copy-start(bf16[768,512]{1,0:T(8,128)(2,1)S(1)} %collective-permute-done.2.refs_3_) | copy-start | bytes 2359300
  82.8 6.5 %collective-permute-start.7 = (bf16[768,512]{1,0:T(8,128)(2,1)S(1)}, bf16[768,512]{1,0:T(8,128)(2,1)S(1)}, u32[]{:S(2)}, u32[]{:S(2)}) collective-permute-start(bf16[768,512]{1,0:T(8,128)(2,1)S(1)} %collective-permute-done.2.refs_3_), channel_id=1, source_target_pairs={{0,1},{1,0},{2,3},{3,2},{4,5},{5,4},{6,7},{7,6},{8,9},{9,8},{10,11... | collective-permute-start | bytes 2359304 | tf_op jit(solution)/shard_map/ppermute | solution.py:241
  87.4 4.2 %copy-start.15 = (bf16[768,512]{1,0:T(8,128)(2,1)}, bf16[768,512]{1,0:T(8,128)(2,1)S(1)}, u32[]{:S(2)}) copy-start(bf16[768,512]{1,0:T(8,128)(2,1)S(1)} %collective-permute-done.3.refs_4_) | copy-start | bytes 2359300
  87.4 4.2 %collective-permute-start.8 = (bf16[768,512]{1,0:T(8,128)(2,1)S(1)}, bf16[768,512]{1,0:T(8,128)(2,1)S(1)}, u32[]{:S(2)}, u32[]{:S(2)}) collective-permute-start(bf16[768,512]{1,0:T(8,128)(2,1)S(1)} %collective-permute-done.3.refs_4_), channel_id=1, source_target_pairs={{0,1},{1,0},{2,3},{3,2},{4,5},{5,4},{6,7},{7,6},{8,9},{9,8},{10,11... | collective-permute-start | bytes 2359304 | tf_op jit(solution)/shard_map/ppermute | solution.py:241
  89.4 2.3 %copy-start.12 = (bf16[1536,512]{1,0:T(8,128)(2,1)}, bf16[1536,512]{1,0:T(8,128)(2,1)S(1)}, u32[]{:S(2)}) copy-start(bf16[1536,512]{1,0:T(8,128)(2,1)S(1)} %collective-permute-done.4.refs_5_) | copy-start | bytes 4718596
  89.4 2.3 %copy-start.16 = (bf16[768,512]{1,0:T(8,128)(2,1)}, bf16[768,512]{1,0:T(8,128)(2,1)S(1)}, u32[]{:S(2)}) copy-start(bf16[768,512]{1,0:T(8,128)(2,1)S(1)} %collective-permute-done.7.refs_8_) | copy-start | bytes 2359300
  91.6 0.9 copy-start.17
  92.5 1.2 copy-start.13
  93.7 1.4 copy-start.8
  108.9 71.0 %copy-start.2 = (bf16[128,512]{1,0:T(8,128)(2,1)S(1)}, bf16[128,512]{1,0:T(8,128)(2,1)}, u32[]{:S(2)}) copy-start(bf16[128,512]{1,0:T(8,128)(2,1)} %get-tuple-element.11.mh_ref) | copy-start | bytes 393220
  108.9 71.0 %copy-start.3 = (bf16[128,512]{1,0:T(8,128)(2,1)S(1)}, bf16[128,512]{1,0:T(8,128)(2,1)}, u32[]{:S(2)}) copy-start(bf16[128,512]{1,0:T(8,128)(2,1)} %get-tuple-element.12.ml_ref) | copy-start | bytes 393220
  108.9 71.0 %copy-start.4 = (bf16[128,64]{1,0:T(8,128)(2,1)S(1)}, bf16[128,64]{1,0:T(8,128)(2,1)}, u32[]{:S(2)}) copy-start(bf16[128,64]{1,0:T(8,128)(2,1)} %get-tuple-element.13.lh_ref) | copy-start | bytes 49156
  108.9 71.0 %copy-start.5 = (bf16[128,64]{1,0:T(8,128)(2,1)S(1)}, bf16[128,64]{1,0:T(8,128)(2,1)}, u32[]{:S(2)}) copy-start(bf16[128,64]{1,0:T(8,128)(2,1)} %get-tuple-element.14.ll_ref) | copy-start | bytes 49156
  108.9 71.0 %copy-start.7 = (s32[2]{0:T(128)S(1)}, s32[2]{0:T(128)}, u32[]{:S(2)}) copy-start(s32[2]{0:T(128)} %pad_add_fusion.where_ref) | copy-start | bytes 28
  179.9 4.9 %copy-start = (bf16[128,2048]{1,0:T(8,128)(2,1)S(1)}, bf16[128,2048]{1,0:T(8,128)(2,1)}, u32[]{:S(2)}) copy-start(bf16[128,2048]{1,0:T(8,128)(2,1)} %state_ref.1) | copy-start | bytes 1572868
  179.9 4.9 %copy-start.1 = (bf16[128,2048]{1,0:T(8,128)(2,1)S(1)}, bf16[128,2048]{1,0:T(8,128)(2,1)}, u32[]{:S(2)}) copy-start(bf16[128,2048]{1,0:T(8,128)(2,1)} %prelude_ref.1) | copy-start | bytes 1572868
  179.9 4.9 %copy-start.6 = (f32[2048]{0:T(1024)S(1)}, f32[2048]{0:T(1024)}, u32[]{:S(2)}) copy-start(f32[2048]{0:T(1024)} %param.11) | copy-start | bytes 24580
  181.1 4.8 %collective-permute-start.9 = (bf16[128,1024]{1,0:T(8,128)(2,1)S(1)}, bf16[128,1024]{1,0:T(8,128)(2,1)S(1)}, u32[]{:S(2)}, u32[]{:S(2)}) collective-permute-start(bf16[128,1024]{1,0:T(8,128)(2,1)S(1)} %shard_map.94), channel_id=1, source_target_pairs={{0,1},{1,0},{2,3},{3,2},{4,5},{5,4},{6,7},{7,6},{8,9},{9,8},{10,11... | collective-permute-start | bytes 786440 | tf_op jit(solution)/shard_map/ppermute | solution.py:278

commit v2 on v1

v2 whole, which is shorter than its diff:
```python
import jax
import jax.numpy as jnp
from jax import lax
from jax.experimental import pallas as pl
from jax.experimental.pallas import tpu as pltpu
from jax.sharding import PartitionSpec as P


TOPK = 8
CAP = 18
MAIN = 8
HALF_CAP = CAP // 2
LANES = 128
AHEAD = 4
WHOLE = 67_000_000
F32 = jnp.float32
BF16 = jnp.bfloat16
VMEM = pl.BlockSpec(memory_space=pltpu.VMEM)
FAR = pl.BlockSpec(memory_space=pltpu.HBM)


def dot(a, b):
    return jnp.dot(a, b, preferred_element_type=F32)


def dot_t(a, b):
    return lax.dot_general(a, b, (((0,), (0,)), ((), ())), preferred_element_type=F32)


def normalize(state, prelude, inject, gain):
    mixed = state.astype(F32) + prelude.astype(F32) * inject
    inv_rms = lax.rsqrt(jnp.mean(mixed * mixed, axis=-1, keepdims=True) + 1e-06)
    return (mixed * inv_rms * gain).astype(BF16)


def places(routes, experts):
    routes = routes.astype(F32).T.astype(jnp.int32)
    tokens = routes.shape[0]
    expert = lax.broadcasted_iota(jnp.int32, (tokens, experts), 1)
    chosen = routes[:, 0:1] == expert
    for k in range(1, TOPK):
        chosen = jnp.logical_or(chosen, routes[:, k : k + 1] == expert)
    earlier = lax.broadcasted_iota(jnp.int32, (tokens, tokens), 1) < lax.broadcasted_iota(
        jnp.int32, (tokens, tokens), 0
    )
    rank = dot(earlier.astype(F32).astype(BF16), chosen.astype(F32).astype(BF16))
    return jnp.where(chosen, rank + 1.0, 0.0)


def widen(rows, times):
    lane = lax.broadcasted_iota(jnp.int32, (rows, rows * times), 1)
    row = lax.broadcasted_iota(jnp.int32, (rows, rows * times), 0)
    return (lane // times == row).astype(F32).astype(BF16)


def route_kernel(*refs):
    stored, parts, out_ref, own_refs = refs[:5], refs[5:8], refs[8], refs[9:11]
    held, send_ref, pack_ref, sems, pack_sems, out_sems, own_sems = (
        refs[11:16], refs[16], refs[17], refs[18], refs[19], refs[20], refs[21],
    )
    copies = [pltpu.make_async_copy(stored[i], held[i], sems.at[i]) for i in range(5)]
    for copy in copies:
        copy.start()
    size = parts[0].shape[0]
    packs = [
        pltpu.make_async_copy(parts[i], pack_ref.at[i * size : (i + 1) * size], pack_sems.at[i])
        for i in range(3)
    ]
    for copy in packs:
        copy.start()
    routes_ref, state_ref, prelude_ref, inject_ref, gain_ref = held
    width = state_ref.shape[1]
    experts = send_ref.shape[0]
    blocks = width // LANES
    low = lax.axis_index("pair").astype(jnp.int32) * HALF_CAP
    copies[0].wait()
    place = places(routes_ref[...], experts)
    slot = lax.broadcasted_iota(jnp.int32, (place.shape[0], experts * MAIN), 1) % MAIN + (1 + low)
    at_main = dot(place.astype(BF16), widen(experts, MAIN)) == slot.astype(F32)
    at_last = place == (low + HALF_CAP).astype(F32)
    pick_main = at_main.astype(F32).astype(BF16)
    pick_last = at_last.astype(F32).astype(BF16)
    for copy in copies[1:]:
        copy.wait()
    normed = normalize(state_ref[...], prelude_ref[...], inject_ref[...], gain_ref[...])
    outs = []

    def give(first, size):
        copy = pltpu.make_async_copy(
            send_ref.at[:, first : first + size, :],
            out_ref.at[:, first : first + size, :],
            out_sems.at[len(outs)],
        )
        copy.start()
        outs.append(copy)

    last = dot_t(pick_last, normed)
    send_ref[:, blocks * MAIN :, :] = last.reshape(experts, blocks, LANES).astype(BF16)
    give(blocks * MAIN, blocks)
    for pair in range(blocks // 2):
        cols = normed[:, pair * 2 * LANES : (pair + 1) * 2 * LANES]
        rows = dot_t(pick_main, cols)
        for j in range(2):
            c = 2 * pair + j
            send_ref[:, c * MAIN : (c + 1) * MAIN, :] = (
                rows[:, j * LANES : (j + 1) * LANES].reshape(experts, MAIN, LANES).astype(BF16)
            )
        give(pair * 2 * MAIN, 2 * MAIN)
        if pair == 0:
            for copy in packs:
                copy.wait()
            cut = own_refs[0].shape[0]
            owns = [
                pltpu.make_async_copy(
                    pack_ref.at[i * cut : (i + 1) * cut], own_refs[i], own_sems.at[i]
                )
                for i in range(2)
            ]
            for copy in owns:
                copy.start()
    for copy in owns:
        copy.wait()
    for copy in outs:
        copy.wait()


def gate_kernel(
    routes_ref, state_ref, prelude_ref, inject_ref, gain_ref, router_ref,
    main_hi_ref, main_lo_ref, last_hi_ref, last_lo_ref,
):
    experts = router_ref.shape[0]
    place = places(routes_ref[...], experts)
    normed = normalize(state_ref[...], prelude_ref[...], inject_ref[...], gain_ref[...])
    logits = lax.dot_general(
        normed, router_ref[...], (((1,), (1,)), ((), ())), preferred_element_type=F32
    )
    picked = jnp.where(place > 0.0, jax.nn.sigmoid(logits), 0.0)
    gate = picked / jnp.sum(picked, axis=1, keepdims=True)
    gate_hi = gate.astype(BF16)
    gate_lo = (gate - gate_hi.astype(F32)).astype(BF16)
    place = place.astype(BF16)
    for hi_ref, lo_ref, each in ((main_hi_ref, main_lo_ref, MAIN), (last_hi_ref, last_lo_ref, 1)):
        spread = widen(experts, 2 * each)
        lane = lax.broadcasted_iota(jnp.int32, hi_ref.shape, 1)
        core = lane // each % 2
        slot = core * HALF_CAP + (lane % each + 1 if each > 1 else HALF_CAP)
        here = dot(place, spread) == slot.astype(F32)
        hi_ref[...] = jnp.where(here, dot(gate_hi, spread), 0.0).astype(BF16)
        lo_ref[...] = jnp.where(here, dot(gate_lo, spread), 0.0).astype(BF16)


def ffn_kernel(*refs):
    stored, out_ref = refs[:17], refs[17]
    x_ref, last_ref, gate_ref, up_ref, act_ref, back_ref, ends_ref, rows_ref = refs[18:26]
    weights, sems, row_sem, out_sems = refs[26:42], refs[42], refs[43], refs[44]
    sections, _, part = x_ref.shape
    experts = rows_ref.shape[0]
    blocks = sections * part // LANES
    per = part // LANES
    main = experts * MAIN
    half = blocks // 2
    here = lax.axis_index("section").astype(jnp.int32)
    step = 256
    at = [lax.rem(here + d, sections) for d in (0, 1, 3, 2)]
    rows_in = pltpu.make_async_copy(stored[0], rows_ref, row_sem)
    copies = [pltpu.make_async_copy(stored[1 + i], weights[i], sems.at[i]) for i in range(16)]
    rows_in.start()
    for copy in copies[:AHEAD]:
        copy.start()
    rows_in.wait()
    last = rows_ref[:, blocks * MAIN :, :].astype(F32).reshape(experts, blocks * LANES)
    for s in range(sections):
        for c in range(per):
            b = s * per + c
            x_ref[s, :main, c * LANES : (c + 1) * LANES] = (
                rows_ref[:, b * MAIN : (b + 1) * MAIN, :].reshape(main, LANES)
            )
        x_ref[s, main:, :] = last[:, s * part : (s + 1) * part].astype(BF16)

    def piece(q, d, first, cols):
        edge = weights[0].shape[0]
        side, row = divmod(first, edge)
        return weights[q * 8 + d * 2 + side][row : row + step, cols]

    for q in range(2):
        for d in range(sections):
            for i in (q * 8 + d * 2, q * 8 + d * 2 + 1):
                copies[i].wait()
                if i + AHEAD < len(copies):
                    copies[i + AHEAD].start()
            for n in range(part // step):
                cols = slice(n * step, (n + 1) * step)
                totals = []
                for which, sum_ref in enumerate((gate_ref, up_ref)):
                    total = None if d == 0 else sum_ref[:, cols]
                    for k in range(part // step):
                        term = dot(
                            x_ref[at[d], :, k * step : (k + 1) * step],
                            piece(q, d, which * part + k * step, cols),
                        )
                        total = term if total is None else total + term
                    if d < sections - 1:
                        sum_ref[:, cols] = total
                    totals.append(total)
                if d == sections - 1:
                    act = jax.nn.silu(totals[0]) * totals[1]
                    act_ref[:, q * part + n * step : q * part + (n + 1) * step] = act.astype(BF16)
    outs = []
    for d in range(sections):
        wide = []
        for n in range(part // step):
            cols = slice(n * step, (n + 1) * step)
            total = None
            for q in range(2):
                partial = None
                for k in range(part // step):
                    term = dot(
                        act_ref[:, q * part + k * step : q * part + (k + 1) * step],
                        piece(q, d, 2 * part + k * step, cols),
                    )
                    partial = term if partial is None else partial + term
                partial = partial.astype(BF16).astype(F32)
                total = partial if total is None else total + partial
            for j in range(step // LANES):
                back_ref[d, :, n * (step // LANES) + j, :, :] = (
                    total[:main, j * LANES : (j + 1) * LANES]
                    .reshape(experts, MAIN, LANES)
                    .astype(BF16)
                )
            wide.append(total[main:])
        last_ref[at[d]] = jnp.concatenate(wide, axis=1).astype(BF16)
        span = pl.ds(at[d] % 2 * per, per)
        copy = pltpu.make_async_copy(
            back_ref.at[d], out_ref.at[:, at[d] // 2, span, :, :], out_sems.at[d]
        )
        copy.start()
        outs.append(copy)
    whole = jnp.concatenate([last_ref[s] for s in range(sections)], axis=1)
    whole = whole.astype(F32).reshape(experts, blocks, LANES).astype(BF16)
    for h in range(2):
        ends_ref[h] = whole[:, h * half : (h + 1) * half, :]
        copy = pltpu.make_async_copy(
            ends_ref.at[h], out_ref.at[:, h, half, :, :], out_sems.at[sections + h]
        )
        copy.start()
        outs.append(copy)
    for copy in outs:
        copy.wait()


def combine_kernel(
    rows_ref, mh_ref, ml_ref, lh_ref, ll_ref, state_ref, prelude_ref, inject_ref, out_ref
):
    width = out_ref.shape[1]
    senders = rows_ref.shape[0]
    half = width // LANES
    cols = pl.ds(pl.multiple_of(lax.axis_index("pair").astype(jnp.int32) * width, width), width)
    mixed = state_ref[:, cols].astype(F32) + prelude_ref[:, cols].astype(F32) * inject_ref[:, cols]
    last = rows_ref[:, half * MAIN :, :].astype(F32).reshape(senders, width).astype(BF16)
    mixed = mixed + (dot(lh_ref[...], last) + dot(ll_ref[...], last))
    for pair in range(half // 2):
        rows = [
            rows_ref[:, c * MAIN : (c + 1) * MAIN, :].reshape(senders * MAIN, LANES)
            for c in (2 * pair, 2 * pair + 1)
        ]
        rows = jnp.concatenate(rows, axis=1)
        span = slice(pair * 2 * LANES, (pair + 1) * 2 * LANES)
        moe = dot(mh_ref[...], rows) + dot(ml_ref[...], rows)
        out_ref[:, span] = (mixed[:, span] + moe).astype(BF16)


def call(kernel, outs, n_in, scratch=(), limit=10 << 20, far=False, far_outs=0):
    kinds = [FAR] * far_outs + [VMEM] * (len(outs) - far_outs)
    return pl.pallas_call(
        kernel,
        out_shape=outs,
        in_specs=[FAR if far else VMEM] * n_in,
        out_specs=tuple(kinds),
        scratch_shapes=list(scratch),
        compiler_params=pltpu.CompilerParams(vmem_limit_bytes=limit),
    )


def one_pass(initial_state, prelude, inject_gain, norm_gain, router, gate_w, up_w, down_w, routes):
    tokens, width = initial_state.shape
    experts = router.shape[1]
    blocks = width // LANES
    sections = lax.axis_size("section")
    part = gate_w.shape[1]
    inject = inject_gain[None, :]
    shape = jax.ShapeDtypeStruct
    dma = pltpu.SemaphoreType.DMA
    slots = experts * HALF_CAP

    message = shape((experts, blocks * HALF_CAP, LANES), BF16)
    piece = shape((3 * part // 2, part), BF16)
    inputs = (routes[0].T, initial_state, prelude, inject, norm_gain[None, :])
    send, own_lo, own_hi = call(
        route_kernel,
        (message, piece, piece),
        8,
        scratch=[
            pltpu.VMEM((TOPK, tokens), jnp.int32),
            pltpu.VMEM((tokens, width), BF16),
            pltpu.VMEM((tokens, width), BF16),
            pltpu.VMEM((1, width), F32),
            pltpu.VMEM((1, width), F32),
            pltpu.VMEM(message.shape, BF16),
            pltpu.VMEM((3 * part, part), BF16),
            dma((5,)),
            dma((3,)),
            dma((blocks // 2 + 1,)),
            dma((2,)),
        ],
        limit=WHOLE,
        far=True,
        far_outs=3,
    )(*inputs, gate_w[0], up_w[0], down_w[0])

    up_ring = [(i, (i + 1) % sections) for i in range(sections)]
    down_ring = [(i, (i - 1) % sections) for i in range(sections)]
    swap = [(0, 1), (1, 0)]

    before_lo = lax.ppermute(own_lo, "section", up_ring)
    after_hi = lax.ppermute(own_hi, "section", down_ring)
    before_hi = lax.ppermute(own_hi, "section", up_ring)
    after_lo = lax.ppermute(own_lo, "section", down_ring)
    far_lo = lax.ppermute(before_lo, "section", up_ring)
    far_hi = lax.ppermute(after_hi, "section", down_ring)
    mine = [own_lo, own_hi, after_lo, after_hi, before_lo, before_hi, far_lo, far_hi]
    other = [lax.ppermute(w, "pair", swap) for w in mine]

    received = lax.all_to_all(send, "expert", split_axis=0, concat_axis=0, tiled=True)
    (back,) = call(
        ffn_kernel,
        (shape((experts, 2, HALF_CAP, blocks // 2, LANES), BF16),),
        17,
        scratch=[
            pltpu.VMEM((sections, slots, part), BF16),
            pltpu.VMEM((sections, experts, part), BF16),
            pltpu.VMEM((slots, part), F32),
            pltpu.VMEM((slots, part), F32),
            pltpu.VMEM((slots, 2 * part), BF16),
            pltpu.VMEM((sections, experts, blocks // sections, MAIN, LANES), BF16),
            pltpu.VMEM((2, experts, blocks // 2, LANES), BF16),
            pltpu.VMEM(message.shape, BF16),
            *[pltpu.VMEM(w.shape, BF16) for w in mine + other],
            dma((16,)),
            dma,
            dma((sections + 2,)),
        ],
        limit=WHOLE,
        far=True,
        far_outs=1,
    )(received, *mine, *other)
    weights = call(
        gate_kernel,
        (shape((tokens, 2 * experts * MAIN), BF16),) * 2
        + (shape((tokens, 2 * experts), BF16),) * 2,
        6,
    )(*inputs, router.T)
    back = back.reshape(2 * experts, blocks // 2 * HALF_CAP, LANES)
    returned = lax.all_to_all(back, ("expert", "pair"), split_axis=0, concat_axis=0, tiled=True)
    (out,) = call(combine_kernel, (shape((tokens, width // 2), BF16),), 8)(
        returned, *weights, initial_state, prelude, inject
    )
    return out


def solution(mesh):
    placed = (
        P(("section", "expert"), None),
        P(("section", "expert"), None),
        P(),
        P(),
        P(),
        P("expert", "section", "pair"),
        P("expert", "section", "pair"),
        P("expert", "pair", "section"),
        P(None, ("section", "expert"), None),
    )
    return jax.shard_map(
        one_pass,
        mesh=mesh,
        in_specs=placed,
        out_specs=P(("section", "expert"), "pair"),
        check_vma=False,
    )
```

time: 187 us -> 180 us (0.963)
  the two profiles are of different devices: /device:TPU:1 before, /device:TPU:8 now
where the time goes in v2:
time: 180 us; the launch traced here: 179 us
  waiting for transfers between devices  84.6 us (47%)
  starting transfers between devices  68 us (38%)
  Pallas kernels  19.4 us (11%)
  local copies, waits for them, and re-layouts  6.5 us (4%)
    all_to_all x1, waiting for transfers between devices, one_pass(): lax.all_to_all(back, ('expert', 'pair'), split_axis=0, concat_axis=0, til...  56 us
    all_to_all x1, starting transfers between devices, one_pass(): lax.all_to_all(send, 'expert', split_axis=0, concat_axis=0, tiled=True)  16.9 us
    ppermute x8, starting transfers between devices, one_pass(): other = [lax.ppermute(w, 'pair', swap) for w in mine]  16.3 us
    all_to_all x1, starting transfers between devices, one_pass(): lax.all_to_all(back, ('expert', 'pair'), split_axis=0, concat_axis=0, til...  13.7 us
    pallas_call x1, Pallas kernels, one_pass(): call(ffn_kernel, (shape((experts, 2, HALF_CAP, blocks // 2, LANES), BF16)...  12.4 us
    ppermute x1, waiting for transfers between devices, one_pass(): far_lo = lax.ppermute(before_lo, 'section', up_ring)  8.56 us
    ppermute x1, waiting for transfers between devices, one_pass(): after_hi = lax.ppermute(own_hi, 'section', down_ring)  7.63 us
    ppermute x1, waiting for transfers between devices, one_pass(): after_lo = lax.ppermute(own_lo, 'section', down_ring)  6.98 us
  transfers between devices with their start and end apart: 16, of which 6 were waited for; matrix products, arithmetic and copies ran while one was open for 0% of the time, Pallas kernels for 1%

profile of v2, /device:TPU:8, one launch (start us, length us, event | category | flops | bytes accessed | tf_op | source)
XLA Modules:
  0.0 179.1 jit_solution(13001468287490784733)
XLA Ops:
  0.0 4.1 %shard_map.91 = (bf16[64,144,128]{2,1,0:T(8,128)(2,1)}, bf16[768,512]{1,0:T(8,128)(2,1)}, bf16[768,512]{1,0:T(8,128)(2,1)}) custom-call(s32[8,128]{1,0:T(8,128)} %bitcast.16, bf16[128,2048]{1,0:T(8,128)(2,1)} %state_ref.3, bf16[128,2048]{1,0:T(8,128)(2,1)} %prelude_ref.3, f32[1,2048]{1,0:T(1,128)} %bitcast.11, f32[1,2048]{1,0:T(1,128)} %bitcast.14, ...), custom_call_target="tpu_custom_call" | custom-call | tf_op jit(solution)/shard_map/pallas_call | solution.py:298
  4.1 16.9 %all-to-all-start = ((bf16[64,144,128]{2,1,0:T(8,128)(2,1)}), bf16[64,144,128]{2,1,0:T(8,128)(2,1)}, u32[]{:S(2)}, u32[]{:S(2)}) async-start(bf16[64,144,128]{2,1,0:T(8,128)(2,1)} %get-tuple-element.12), calls=%async_computation | async-start | bytes 4718592 | tf_op jit(solution)/shard_map/all_to_all | solution.py:333
  21.0 4.7 %collective-permute-start = (bf16[768,512]{1,0:T(8,128)(2,1)S(1)}, bf16[768,512]{1,0:T(8,128)(2,1)S(1)}, u32[]{:S(2)}, u32[]{:S(2)}) collective-permute-start(bf16[768,512]{1,0:T(8,128)(2,1)S(1)} %copy-done.10), channel_id=1, source_target_pairs={{0,384},{128,0},{256,128},{384,256},{1,385},{129,1},{257,129},{385... | collective-permute-start | bytes 2359304 | tf_op jit(solution)/shard_map/ppermute | solution.py:327
  25.7 1.9 %collective-permute-start.2 = (bf16[768,512]{1,0:T(8,128)(2,1)S(1)}, bf16[768,512]{1,0:T(8,128)(2,1)S(1)}, u32[]{:S(2)}, u32[]{:S(2)}) collective-permute-start(bf16[768,512]{1,0:T(8,128)(2,1)S(1)} %copy-done.10), channel_id=1, source_target_pairs={{0,128},{128,256},{256,384},{384,0},{1,129},{129,257},{257,385},{3... | collective-permute-start | bytes 2359304 | tf_op jit(solution)/shard_map/ppermute | solution.py:324
  27.6 5.1 %collective-permute-start.1 = (bf16[768,512]{1,0:T(8,128)(2,1)S(1)}, bf16[768,512]{1,0:T(8,128)(2,1)S(1)}, u32[]{:S(2)}, u32[]{:S(2)}) collective-permute-start(bf16[768,512]{1,0:T(8,128)(2,1)S(1)} %copy-done.11), channel_id=1, source_target_pairs={{0,384},{128,0},{256,128},{384,256},{1,385},{129,1},{257,129},{385... | collective-permute-start | bytes 2359304 | tf_op jit(solution)/shard_map/ppermute | solution.py:325
  32.8 1.9 %collective-permute-start.3 = (bf16[768,512]{1,0:T(8,128)(2,1)S(1)}, bf16[768,512]{1,0:T(8,128)(2,1)S(1)}, u32[]{:S(2)}, u32[]{:S(2)}) collective-permute-start(bf16[768,512]{1,0:T(8,128)(2,1)S(1)} %copy-done.11), channel_id=1, source_target_pairs={{0,128},{128,256},{256,384},{384,0},{1,129},{129,257},{257,385},{3... | collective-permute-start | bytes 2359304 | tf_op jit(solution)/shard_map/ppermute | solution.py:326
  34.7 1.9 %collective-permute-start.6 = (bf16[768,512]{1,0:T(8,128)(2,1)S(1)}, bf16[768,512]{1,0:T(8,128)(2,1)S(1)}, u32[]{:S(2)}, u32[]{:S(2)}) collective-permute-start(bf16[768,512]{1,0:T(8,128)(2,1)S(1)} %copy-done.10), channel_id=1, source_target_pairs={{0,1},{1,0},{2,3},{3,2},{4,5},{5,4},{6,7},{7,6},{8,9},{9,8},{10,11... | collective-permute-start | bytes 2359304 | tf_op jit(solution)/shard_map/ppermute | solution.py:331
  36.6 7.0 %collective-permute-done.refs_3_ = bf16[768,512]{1,0:T(8,128)(2,1)S(1)} collective-permute-done((bf16[768,512]{1,0:T(8,128)(2,1)S(1)}, bf16[768,512]{1,0:T(8,128)(2,1)S(1)}, u32[]{:S(2)}, u32[]{:S(2)}) %collective-permute-start) | collective-permute-done | bytes 786464 | tf_op jit(solution)/shard_map/ppermute | solution.py:327
  43.6 1.9 %collective-permute-start.7 = (bf16[768,512]{1,0:T(8,128)(2,1)S(1)}, bf16[768,512]{1,0:T(8,128)(2,1)S(1)}, u32[]{:S(2)}, u32[]{:S(2)}) collective-permute-start(bf16[768,512]{1,0:T(8,128)(2,1)S(1)} %copy-done.11), channel_id=1, source_target_pairs={{0,1},{1,0},{2,3},{3,2},{4,5},{5,4},{6,7},{7,6},{8,9},{9,8},{10,11... | collective-permute-start | bytes 2359304 | tf_op jit(solution)/shard_map/ppermute | solution.py:331
  45.5 3.7 %collective-permute-done.2.refs_5_ = bf16[768,512]{1,0:T(8,128)(2,1)S(1)} collective-permute-done((bf16[768,512]{1,0:T(8,128)(2,1)S(1)}, bf16[768,512]{1,0:T(8,128)(2,1)S(1)}, u32[]{:S(2)}, u32[]{:S(2)}) %collective-permute-start.2) | collective-permute-done | bytes 786464 | tf_op jit(solution)/shard_map/ppermute | solution.py:324
  49.2 1.9 %collective-permute-start.4 = (bf16[768,512]{1,0:T(8,128)(2,1)S(1)}, bf16[768,512]{1,0:T(8,128)(2,1)S(1)}, u32[]{:S(2)}, u32[]{:S(2)}) collective-permute-start(bf16[768,512]{1,0:T(8,128)(2,1)S(1)} %collective-permute-done.2.refs_5_), channel_id=1, source_target_pairs={{0,128},{128,256},{256,384},{384,0},{1,129},{129,257},{257,385},{3... | collective-permute-start | bytes 2359304 | tf_op jit(solution)/shard_map/ppermute | solution.py:328
  51.1 7.6 %collective-permute-done.1.refs_4_ = bf16[768,512]{1,0:T(8,128)(2,1)S(1)} collective-permute-done((bf16[768,512]{1,0:T(8,128)(2,1)S(1)}, bf16[768,512]{1,0:T(8,128)(2,1)S(1)}, u32[]{:S(2)}, u32[]{:S(2)}) %collective-permute-start.1) | collective-permute-done | bytes 786464 | tf_op jit(solution)/shard_map/ppermute | solution.py:325
  58.8 5.6 %collective-permute-start.5 = (bf16[768,512]{1,0:T(8,128)(2,1)S(1)}, bf16[768,512]{1,0:T(8,128)(2,1)S(1)}, u32[]{:S(2)}, u32[]{:S(2)}) collective-permute-start(bf16[768,512]{1,0:T(8,128)(2,1)S(1)} %collective-permute-done.1.refs_4_), channel_id=1, source_target_pairs={{0,384},{128,0},{256,128},{384,256},{1,385},{129,1},{257,129},{385... | collective-permute-start | bytes 2359304 | tf_op jit(solution)/shard_map/ppermute | solution.py:329
  64.4 1.7 collective-permute-done.3.refs_6_
  66.1 1.9 %collective-permute-start.8 = (bf16[768,512]{1,0:T(8,128)(2,1)S(1)}, bf16[768,512]{1,0:T(8,128)(2,1)S(1)}, u32[]{:S(2)}, u32[]{:S(2)}) collective-permute-start(bf16[768,512]{1,0:T(8,128)(2,1)S(1)} %collective-permute-done.refs_3_), channel_id=1, source_target_pairs={{0,1},{1,0},{2,3},{3,2},{4,5},{5,4},{6,7},{7,6},{8,9},{9,8},{10,11... | collective-permute-start | bytes 2359304 | tf_op jit(solution)/shard_map/ppermute | solution.py:331
  68.0 2.4 %collective-permute-start.9 = (bf16[768,512]{1,0:T(8,128)(2,1)S(1)}, bf16[768,512]{1,0:T(8,128)(2,1)S(1)}, u32[]{:S(2)}, u32[]{:S(2)}) collective-permute-start(bf16[768,512]{1,0:T(8,128)(2,1)S(1)} %collective-permute-done.1.refs_4_), channel_id=1, source_target_pairs={{0,1},{1,0},{2,3},{3,2},{4,5},{5,4},{6,7},{7,6},{8,9},{9,8},{10,11... | collective-permute-start | bytes 2359304 | tf_op jit(solution)/shard_map/ppermute | solution.py:331
  70.4 1.9 %collective-permute-start.10 = (bf16[768,512]{1,0:T(8,128)(2,1)S(1)}, bf16[768,512]{1,0:T(8,128)(2,1)S(1)}, u32[]{:S(2)}, u32[]{:S(2)}) collective-permute-start(bf16[768,512]{1,0:T(8,128)(2,1)S(1)} %collective-permute-done.2.refs_5_), channel_id=1, source_target_pairs={{0,1},{1,0},{2,3},{3,2},{4,5},{5,4},{6,7},{7,6},{8,9},{9,8},{10,11... | collective-permute-start | bytes 2359304 | tf_op jit(solution)/shard_map/ppermute | solution.py:331
  72.4 8.6 %collective-permute-done.4.refs_7_ = bf16[768,512]{1,0:T(8,128)(2,1)S(1)} collective-permute-done((bf16[768,512]{1,0:T(8,128)(2,1)S(1)}, bf16[768,512]{1,0:T(8,128)(2,1)S(1)}, u32[]{:S(2)}, u32[]{:S(2)}) %collective-permute-start.4) | collective-permute-done | bytes 786464 | tf_op jit(solution)/shard_map/ppermute | solution.py:328
  80.9 1.9 %collective-permute-start.11 = (bf16[768,512]{1,0:T(8,128)(2,1)S(1)}, bf16[768,512]{1,0:T(8,128)(2,1)S(1)}, u32[]{:S(2)}, u32[]{:S(2)}) collective-permute-start(bf16[768,512]{1,0:T(8,128)(2,1)S(1)} %collective-permute-done.3.refs_6_), channel_id=1, source_target_pairs={{0,1},{1,0},{2,3},{3,2},{4,5},{5,4},{6,7},{7,6},{8,9},{9,8},{10,11... | collective-permute-start | bytes 2359304 | tf_op jit(solution)/shard_map/ppermute | solution.py:331
  82.9 2.4 %collective-permute-start.12 = (bf16[768,512]{1,0:T(8,128)(2,1)S(1)}, bf16[768,512]{1,0:T(8,128)(2,1)S(1)}, u32[]{:S(2)}, u32[]{:S(2)}) collective-permute-start(bf16[768,512]{1,0:T(8,128)(2,1)S(1)} %collective-permute-done.4.refs_7_), channel_id=1, source_target_pairs={{0,1},{1,0},{2,3},{3,2},{4,5},{5,4},{6,7},{7,6},{8,9},{9,8},{10,11... | collective-permute-start | bytes 2359304 | tf_op jit(solution)/shard_map/ppermute | solution.py:331
  85.3 1.9 %collective-permute-start.13 = (bf16[768,512]{1,0:T(8,128)(2,1)S(1)}, bf16[768,512]{1,0:T(8,128)(2,1)}, u32[]{:S(2)}, u32[]{:S(2)}) collective-permute-start(bf16[768,512]{1,0:T(8,128)(2,1)S(1)} %collective-permute-done.5.refs_8_), channel_id=1, source_target_pairs={{0,1},{1,0},{2,3},{3,2},{4,5},{5,4},{6,7},{7,6},{8,9},{9,8},{10,11... | collective-permute-start | bytes 2359304 | tf_op jit(solution)/shard_map/ppermute | solution.py:331
  87.4 0.7 copy-done.21
  88.7 0.9 copy-done.24
  89.6 12.4 %shard_map.92 = bf16[64,2,9,8,128]{4,3,2,1,0:T(8,128)(2,1)} custom-call(bf16[64,144,128]{2,1,0:T(8,128)(2,1)} %all-to-all-done.refs_0_, bf16[768,512]{1,0:T(8,128)(2,1)} %get-tuple-element.13.refs_1_, bf16[768,512]{1,0:T(8,128)(2,1)} %get-tuple-element.14.refs_2_, bf16[768,512]{1,0:T(8,128)(2,1)} %copy-done.12, bf16[768,512]{1,0:T(8,128)(2,1)} %copy-done.14, ...), custom_call_target="tpu_custom_call" | custom-call | tf_op jit(solution)/shard_map/pallas_call | solution.py:334
  102.2 13.7 %all-to-all-start.1 = ((bf16[128,72,128]{2,1,0:T(8,128)(2,1)}), bf16[128,72,128]{2,1,0:T(8,128)(2,1)S(1)}, u32[]{:S(2)}, u32[]{:S(2)}) async-start(bf16[128,72,128]{2,1,0:T(8,128)(2,1)} %bitcast.18), calls=%async_computation.1 | async-start | bytes 4718592 | tf_op jit(solution)/shard_map/all_to_all | solution.py:363
  115.9 0.9 copy-done.6
  116.8 1.2 shard_map.93
  118.1 0.7 copy-done.2
  119.5 56.0 %all-to-all-done.1.rows_ref = bf16[128,72,128]{2,1,0:T(8,128)(2,1)S(1)} async-done(((bf16[128,72,128]{2,1,0:T(8,128)(2,1)}), bf16[128,72,128]{2,1,0:T(8,128)(2,1)S(1)}, u32[]{:S(2)}, u32[]{:S(2)}) %all-to-all-start.1) | async-done | bytes 2359328 | tf_op jit(solution)/shard_map/all_to_all | solution.py:363
  175.5 0.9 copy-done.3
  176.4 0.9 copy-done.5
  177.4 1.7 shard_map.94
  (54 shorter events, 1.4 us)
Async XLA Ops:
  4.1 16.9 %copy-start.10 = (bf16[768,512]{1,0:T(8,128)(2,1)S(1)}, bf16[768,512]{1,0:T(8,128)(2,1)}, u32[]{:S(2)}) copy-start(bf16[768,512]{1,0:T(8,128)(2,1)} %get-tuple-element.13.refs_1_) | copy-start | bytes 2359300
  4.1 23.5 %copy-start.11 = (bf16[768,512]{1,0:T(8,128)(2,1)S(1)}, bf16[768,512]{1,0:T(8,128)(2,1)}, u32[]{:S(2)}) copy-start(bf16[768,512]{1,0:T(8,128)(2,1)} %get-tuple-element.14.refs_2_) | copy-start | bytes 2359300
  4.1 85.5 %all-to-all-start = ((bf16[64,144,128]{2,1,0:T(8,128)(2,1)}), bf16[64,144,128]{2,1,0:T(8,128)(2,1)}, u32[]{:S(2)}, u32[]{:S(2)}) async-start(bf16[64,144,128]{2,1,0:T(8,128)(2,1)} %get-tuple-element.12), calls=%async_computation | async-start | bytes 4718592 | tf_op jit(solution)/shard_map/all_to_all | solution.py:333
  21.0 22.6 %collective-permute-start = (bf16[768,512]{1,0:T(8,128)(2,1)S(1)}, bf16[768,512]{1,0:T(8,128)(2,1)S(1)}, u32[]{:S(2)}, u32[]{:S(2)}) collective-permute-start(bf16[768,512]{1,0:T(8,128)(2,1)S(1)} %copy-done.10), channel_id=1, source_target_pairs={{0,384},{128,0},{256,128},{384,256},{1,385},{129,1},{257,129},{385... | collective-permute-start | bytes 2359304 | tf_op jit(solution)/shard_map/ppermute | solution.py:327
  25.7 23.5 %collective-permute-start.2 = (bf16[768,512]{1,0:T(8,128)(2,1)S(1)}, bf16[768,512]{1,0:T(8,128)(2,1)S(1)}, u32[]{:S(2)}, u32[]{:S(2)}) collective-permute-start(bf16[768,512]{1,0:T(8,128)(2,1)S(1)} %copy-done.10), channel_id=1, source_target_pairs={{0,128},{128,256},{256,384},{384,0},{1,129},{129,257},{257,385},{3... | collective-permute-start | bytes 2359304 | tf_op jit(solution)/shard_map/ppermute | solution.py:324
  27.6 31.1 %collective-permute-start.1 = (bf16[768,512]{1,0:T(8,128)(2,1)S(1)}, bf16[768,512]{1,0:T(8,128)(2,1)S(1)}, u32[]{:S(2)}, u32[]{:S(2)}) collective-permute-start(bf16[768,512]{1,0:T(8,128)(2,1)S(1)} %copy-done.11), channel_id=1, source_target_pairs={{0,384},{128,0},{256,128},{384,256},{1,385},{129,1},{257,129},{385... | collective-permute-start | bytes 2359304 | tf_op jit(solution)/shard_map/ppermute | solution.py:325
  32.8 33.3 %collective-permute-start.3 = (bf16[768,512]{1,0:T(8,128)(2,1)S(1)}, bf16[768,512]{1,0:T(8,128)(2,1)S(1)}, u32[]{:S(2)}, u32[]{:S(2)}) collective-permute-start(bf16[768,512]{1,0:T(8,128)(2,1)S(1)} %copy-done.11), channel_id=1, source_target_pairs={{0,128},{128,256},{256,384},{384,0},{1,129},{129,257},{257,385},{3... | collective-permute-start | bytes 2359304 | tf_op jit(solution)/shard_map/ppermute | solution.py:326
  34.7 33.3 %collective-permute-start.6 = (bf16[768,512]{1,0:T(8,128)(2,1)S(1)}, bf16[768,512]{1,0:T(8,128)(2,1)S(1)}, u32[]{:S(2)}, u32[]{:S(2)}) collective-permute-start(bf16[768,512]{1,0:T(8,128)(2,1)S(1)} %copy-done.10), channel_id=1, source_target_pairs={{0,1},{1,0},{2,3},{3,2},{4,5},{5,4},{6,7},{7,6},{8,9},{9,8},{10,11... | collective-permute-start | bytes 2359304 | tf_op jit(solution)/shard_map/ppermute | solution.py:331
  43.6 26.8 %copy-start.12 = (bf16[768,512]{1,0:T(8,128)(2,1)}, bf16[768,512]{1,0:T(8,128)(2,1)S(1)}, u32[]{:S(2)}) copy-start(bf16[768,512]{1,0:T(8,128)(2,1)S(1)} %collective-permute-done.refs_3_) | copy-start | bytes 2359300
  43.6 26.8 %collective-permute-start.7 = (bf16[768,512]{1,0:T(8,128)(2,1)S(1)}, bf16[768,512]{1,0:T(8,128)(2,1)S(1)}, u32[]{:S(2)}, u32[]{:S(2)}) collective-permute-start(bf16[768,512]{1,0:T(8,128)(2,1)S(1)} %copy-done.11), channel_id=1, source_target_pairs={{0,1},{1,0},{2,3},{3,2},{4,5},{5,4},{6,7},{7,6},{8,9},{9,8},{10,11... | collective-permute-start | bytes 2359304 | tf_op jit(solution)/shard_map/ppermute | solution.py:331
  49.2 36.1 %copy-start.13 = (bf16[768,512]{1,0:T(8,128)(2,1)}, bf16[768,512]{1,0:T(8,128)(2,1)S(1)}, u32[]{:S(2)}) copy-start(bf16[768,512]{1,0:T(8,128)(2,1)S(1)} %collective-permute-done.2.refs_5_) | copy-start | bytes 2359300
  49.2 31.7 %collective-permute-start.4 = (bf16[768,512]{1,0:T(8,128)(2,1)S(1)}, bf16[768,512]{1,0:T(8,128)(2,1)S(1)}, u32[]{:S(2)}, u32[]{:S(2)}) collective-permute-start(bf16[768,512]{1,0:T(8,128)(2,1)S(1)} %collective-permute-done.2.refs_5_), channel_id=1, source_target_pairs={{0,128},{128,256},{256,384},{384,0},{1,129},{129,257},{257,385},{3... | collective-permute-start | bytes 2359304 | tf_op jit(solution)/shard_map/ppermute | solution.py:328
  58.8 28.5 %copy-start.14 = (bf16[768,512]{1,0:T(8,128)(2,1)}, bf16[768,512]{1,0:T(8,128)(2,1)S(1)}, u32[]{:S(2)}) copy-start(bf16[768,512]{1,0:T(8,128)(2,1)S(1)} %collective-permute-done.1.refs_4_) | copy-start | bytes 2359300
  58.8 24.1 %collective-permute-start.5 = (bf16[768,512]{1,0:T(8,128)(2,1)S(1)}, bf16[768,512]{1,0:T(8,128)(2,1)S(1)}, u32[]{:S(2)}, u32[]{:S(2)}) collective-permute-start(bf16[768,512]{1,0:T(8,128)(2,1)S(1)} %collective-permute-done.1.refs_4_), channel_id=1, source_target_pairs={{0,384},{128,0},{256,128},{384,256},{1,385},{129,1},{257,129},{385... | collective-permute-start | bytes 2359304 | tf_op jit(solution)/shard_map/ppermute | solution.py:329
  66.1 21.3 %copy-start.15 = (bf16[768,512]{1,0:T(8,128)(2,1)}, bf16[768,512]{1,0:T(8,128)(2,1)S(1)}, u32[]{:S(2)}) copy-start(bf16[768,512]{1,0:T(8,128)(2,1)S(1)} %collective-permute-done.3.refs_6_) | copy-start | bytes 2359300
  66.1 19.2 %collective-permute-start.8 = (bf16[768,512]{1,0:T(8,128)(2,1)S(1)}, bf16[768,512]{1,0:T(8,128)(2,1)S(1)}, u32[]{:S(2)}, u32[]{:S(2)}) collective-permute-start(bf16[768,512]{1,0:T(8,128)(2,1)S(1)} %collective-permute-done.refs_3_), channel_id=1, source_target_pairs={{0,1},{1,0},{2,3},{3,2},{4,5},{5,4},{6,7},{7,6},{8,9},{9,8},{10,11... | collective-permute-start | bytes 2359304 | tf_op jit(solution)/shard_map/ppermute | solution.py:331
  68.0 19.4 %copy-start.16 = (bf16[768,512]{1,0:T(8,128)(2,1)}, bf16[768,512]{1,0:T(8,128)(2,1)S(1)}, u32[]{:S(2)}) copy-start(bf16[768,512]{1,0:T(8,128)(2,1)S(1)} %collective-permute-done.6.refs_9_) | copy-start | bytes 2359300
  68.0 19.3 %collective-permute-start.9 = (bf16[768,512]{1,0:T(8,128)(2,1)S(1)}, bf16[768,512]{1,0:T(8,128)(2,1)S(1)}, u32[]{:S(2)}, u32[]{:S(2)}) collective-permute-start(bf16[768,512]{1,0:T(8,128)(2,1)S(1)} %collective-permute-done.1.refs_4_), channel_id=1, source_target_pairs={{0,1},{1,0},{2,3},{3,2},{4,5},{5,4},{6,7},{7,6},{8,9},{9,8},{10,11... | collective-permute-start | bytes 2359304 | tf_op jit(solution)/shard_map/ppermute | solution.py:331
  70.4 16.9 %copy-start.17 = (bf16[768,512]{1,0:T(8,128)(2,1)}, bf16[768,512]{1,0:T(8,128)(2,1)S(1)}, u32[]{:S(2)}) copy-start(bf16[768,512]{1,0:T(8,128)(2,1)S(1)} %collective-permute-done.7.refs_10_) | copy-start | bytes 2359300
  70.4 16.8 %collective-permute-start.10 = (bf16[768,512]{1,0:T(8,128)(2,1)S(1)}, bf16[768,512]{1,0:T(8,128)(2,1)S(1)}, u32[]{:S(2)}, u32[]{:S(2)}) collective-permute-start(bf16[768,512]{1,0:T(8,128)(2,1)S(1)} %collective-permute-done.2.refs_5_), channel_id=1, source_target_pairs={{0,1},{1,0},{2,3},{3,2},{4,5},{5,4},{6,7},{7,6},{8,9},{9,8},{10,11... | collective-permute-start | bytes 2359304 | tf_op jit(solution)/shard_map/ppermute | solution.py:331
  80.9 6.4 %copy-start.18 = (bf16[768,512]{1,0:T(8,128)(2,1)}, bf16[768,512]{1,0:T(8,128)(2,1)S(1)}, u32[]{:S(2)}) copy-start(bf16[768,512]{1,0:T(8,128)(2,1)S(1)} %collective-permute-done.4.refs_7_) | copy-start | bytes 2359300
  80.9 6.4 %collective-permute-start.11 = (bf16[768,512]{1,0:T(8,128)(2,1)S(1)}, bf16[768,512]{1,0:T(8,128)(2,1)S(1)}, u32[]{:S(2)}, u32[]{:S(2)}) collective-permute-start(bf16[768,512]{1,0:T(8,128)(2,1)S(1)} %collective-permute-done.3.refs_6_), channel_id=1, source_target_pairs={{0,1},{1,0},{2,3},{3,2},{4,5},{5,4},{6,7},{7,6},{8,9},{9,8},{10,11... | collective-permute-start | bytes 2359304 | tf_op jit(solution)/shard_map/ppermute | solution.py:331
  82.9 4.5 %copy-start.19 = (bf16[768,512]{1,0:T(8,128)(2,1)}, bf16[768,512]{1,0:T(8,128)(2,1)S(1)}, u32[]{:S(2)}) copy-start(bf16[768,512]{1,0:T(8,128)(2,1)S(1)} %collective-permute-done.5.refs_8_) | copy-start | bytes 2359300
  82.9 4.5 %collective-permute-start.12 = (bf16[768,512]{1,0:T(8,128)(2,1)S(1)}, bf16[768,512]{1,0:T(8,128)(2,1)S(1)}, u32[]{:S(2)}, u32[]{:S(2)}) collective-permute-start(bf16[768,512]{1,0:T(8,128)(2,1)S(1)} %collective-permute-done.4.refs_7_), channel_id=1, source_target_pairs={{0,1},{1,0},{2,3},{3,2},{4,5},{5,4},{6,7},{7,6},{8,9},{9,8},{10,11... | collective-permute-start | bytes 2359304 | tf_op jit(solution)/shard_map/ppermute | solution.py:331
  85.3 2.1 %copy-start.20 = (bf16[768,512]{1,0:T(8,128)(2,1)}, bf16[768,512]{1,0:T(8,128)(2,1)S(1)}, u32[]{:S(2)}) copy-start(bf16[768,512]{1,0:T(8,128)(2,1)S(1)} %collective-permute-done.8.refs_11_) | copy-start | bytes 2359300
  85.3 4.3 %collective-permute-start.13 = (bf16[768,512]{1,0:T(8,128)(2,1)S(1)}, bf16[768,512]{1,0:T(8,128)(2,1)}, u32[]{:S(2)}, u32[]{:S(2)}) collective-permute-start(bf16[768,512]{1,0:T(8,128)(2,1)S(1)} %collective-permute-done.5.refs_8_), channel_id=1, source_target_pairs={{0,1},{1,0},{2,3},{3,2},{4,5},{5,4},{6,7},{7,6},{8,9},{9,8},{10,11... | collective-permute-start | bytes 2359304 | tf_op jit(solution)/shard_map/ppermute | solution.py:331
  102.1 13.7 %copy-start = (bf16[128,2048]{1,0:T(8,128)(2,1)S(1)}, bf16[128,2048]{1,0:T(8,128)(2,1)}, u32[]{:S(2)}) copy-start(bf16[128,2048]{1,0:T(8,128)(2,1)} %state_ref.3) | copy-start | bytes 1572868
  102.1 13.7 %copy-start.1 = (bf16[128,2048]{1,0:T(8,128)(2,1)S(1)}, bf16[128,2048]{1,0:T(8,128)(2,1)}, u32[]{:S(2)}) copy-start(bf16[128,2048]{1,0:T(8,128)(2,1)} %prelude_ref.3) | copy-start | bytes 1572868
  102.1 13.7 %copy-start.7 = (f32[2048]{0:T(1024)S(1)}, f32[2048]{0:T(1024)}, u32[]{:S(2)}) copy-start(f32[2048]{0:T(1024)} %param.11) | copy-start | bytes 24580
  102.1 13.7 %copy-start.8 = (f32[2048]{0:T(1024)S(1)}, f32[2048]{0:T(1024)}, u32[]{:S(2)}) copy-start(f32[2048]{0:T(1024)} %param.12) | copy-start | bytes 24580
  102.1 13.7 %copy-start.9 = (s32[1,128,8]{1,2,0:T(8,128)S(1)}, s32[1,128,8]{1,2,0:T(8,128)}, u32[]{:S(2)}) copy-start(s32[1,128,8]{1,2,0:T(8,128)} %param.17) | copy-start | bytes 12292
  102.2 73.3 %all-to-all-start.1 = ((bf16[128,72,128]{2,1,0:T(8,128)(2,1)}), bf16[128,72,128]{2,1,0:T(8,128)(2,1)S(1)}, u32[]{:S(2)}, u32[]{:S(2)}) async-start(bf16[128,72,128]{2,1,0:T(8,128)(2,1)} %bitcast.18), calls=%async_computation.1 | async-start | bytes 4718592 | tf_op jit(solution)/shard_map/all_to_all | solution.py:363
  (9 other events, 8.5 us)

commit v3 on v2

--- a/solution.py
+++ b/solution.py
@@ -54,9 +54,9 @@
 
 
 def route_kernel(*refs):
-    stored, parts, out_ref, own_refs = refs[:5], refs[5:8], refs[8], refs[9:11]
-    held, send_ref, pack_ref, sems, pack_sems, out_sems, own_sems = (
-        refs[11:16], refs[16], refs[17], refs[18], refs[19], refs[20], refs[21],
+    stored, parts, out_ref, own_ref = refs[:5], refs[5:8], refs[8], refs[9]
+    held, send_ref, pack_ref, sems, pack_sems, out_sems, own_sem = (
+        refs[10:15], refs[15], refs[16], refs[17], refs[18], refs[19], refs[20],
     )
     copies = [pltpu.make_async_copy(stored[i], held[i], sems.at[i]) for i in range(5)]
     for copy in copies:
@@ -109,17 +109,9 @@
         if pair == 0:
             for copy in packs:
                 copy.wait()
-            cut = own_refs[0].shape[0]
-            owns = [
-                pltpu.make_async_copy(
-                    pack_ref.at[i * cut : (i + 1) * cut], own_refs[i], own_sems.at[i]
-                )
-                for i in range(2)
-            ]
-            for copy in owns:
-                copy.start()
-    for copy in owns:
-        copy.wait()
+            own = pltpu.make_async_copy(pack_ref, own_ref, own_sem)
+            own.start()
+    own.wait()
     for copy in outs:
         copy.wait()
 
@@ -150,9 +142,9 @@
 
 
 def ffn_kernel(*refs):
-    stored, out_ref = refs[:17], refs[17]
-    x_ref, last_ref, gate_ref, up_ref, act_ref, back_ref, ends_ref, rows_ref = refs[18:26]
-    weights, sems, row_sem, out_sems = refs[26:42], refs[42], refs[43], refs[44]
+    stored, out_ref = refs[:9], refs[9]
+    x_ref, last_ref, gate_ref, up_ref, act_ref, back_ref, ends_ref, rows_ref = refs[10:18]
+    weights, sems, row_sem, out_sems = refs[18:26], refs[26], refs[27], refs[28]
     sections, _, part = x_ref.shape
     experts = rows_ref.shape[0]
     blocks = sections * part // LANES
@@ -161,9 +153,20 @@
     half = blocks // 2
     here = lax.axis_index("section").astype(jnp.int32)
     step = 256
-    at = [lax.rem(here + d, sections) for d in (0, 1, 3, 2)]
+    turn = 1 - 2 * lax.axis_index("pair").astype(jnp.int32)
+    steps = (0, sections - turn, sections + turn, 2)
+    at = [lax.rem(here + d, sections) for d in steps]
+    same = (0, 2, 1, 3)
+    cut = weights[0].shape[0] // 2
     rows_in = pltpu.make_async_copy(stored[0], rows_ref, row_sem)
-    copies = [pltpu.make_async_copy(stored[1 + i], weights[i], sems.at[i]) for i in range(16)]
+    copies = [
+        pltpu.make_async_copy(
+            stored[1 + i // 2].at[i % 2 * cut : (i % 2 + 1) * cut],
+            weights[i // 2].at[i % 2 * cut : (i % 2 + 1) * cut],
+            sems.at[i],
+        )
+        for i in range(16)
+    ]
     rows_in.start()
     for copy in copies[:AHEAD]:
         copy.start()
@@ -178,9 +181,7 @@
         x_ref[s, main:, :] = last[:, s * part : (s + 1) * part].astype(BF16)
 
     def piece(q, d, first, cols):
-        edge = weights[0].shape[0]
-        side, row = divmod(first, edge)
-        return weights[q * 8 + d * 2 + side][row : row + step, cols]
+        return weights[q * 4 + d][first : first + step, cols]
 
     for q in range(2):
         for d in range(sections):
@@ -195,7 +196,7 @@
                     total = None if d == 0 else sum_ref[:, cols]
                     for k in range(part // step):
                         term = dot(
-                            x_ref[at[d], :, k * step : (k + 1) * step],
+                            x_ref[at[d if q == 0 else same[d]], :, k * step : (k + 1) * step],
                             piece(q, d, which * part + k * step, cols),
                         )
                         total = term if total is None else total + term
@@ -216,7 +217,7 @@
                 for k in range(part // step):
                     term = dot(
                         act_ref[:, q * part + k * step : q * part + (k + 1) * step],
-                        piece(q, d, 2 * part + k * step, cols),
+                        piece(q, d if q == 0 else same[d], 2 * part + k * step, cols),
                     )
                     partial = term if partial is None else partial + term
                 partial = partial.astype(BF16).astype(F32)
@@ -293,11 +294,11 @@
     slots = experts * HALF_CAP
 
     message = shape((experts, blocks * HALF_CAP, LANES), BF16)
-    piece = shape((3 * part // 2, part), BF16)
+    piece = shape((3 * part, part), BF16)
     inputs = (routes[0].T, initial_state, prelude, inject, norm_gain[None, :])
-    send, own_lo, own_hi = call(
+    send, own = call(
         route_kernel,
-        (message, piece, piece),
+        (message, piece),
         8,
         scratch=[
             pltpu.VMEM((TOPK, tokens), jnp.int32),
@@ -310,31 +311,31 @@
             dma((5,)),
             dma((3,)),
             dma((blocks // 2 + 1,)),
-            dma((2,)),
+            dma,
         ],
         limit=WHOLE,
         far=True,
-        far_outs=3,
+        far_outs=2,
     )(*inputs, gate_w[0], up_w[0], down_w[0])
 
-    up_ring = [(i, (i + 1) % sections) for i in range(sections)]
-    down_ring = [(i, (i - 1) % sections) for i in range(sections)]
-    swap = [(0, 1), (1, 0)]
-
-    before_lo = lax.ppermute(own_lo, "section", up_ring)
-    after_hi = lax.ppermute(own_hi, "section", down_ring)
-    before_hi = lax.ppermute(own_hi, "section", up_ring)
-    after_lo = lax.ppermute(own_lo, "section", down_ring)
-    far_lo = lax.ppermute(before_lo, "section", up_ring)
-    far_hi = lax.ppermute(after_hi, "section", down_ring)
-    mine = [own_lo, own_hi, after_lo, after_hi, before_lo, before_hi, far_lo, far_hi]
-    other = [lax.ppermute(w, "pair", swap) for w in mine]
+    def ring(turn):
+        return [
+            (2 * i + p, (i + turn * (1 - 2 * p)) % sections * 2 + p)
+            for i in range(sections)
+            for p in range(2)
+        ]
+
+    near = lax.ppermute(own, ("section", "pair"), ring(1))
+    back_near = lax.ppermute(own, ("section", "pair"), ring(-1))
+    far = lax.ppermute(near, ("section", "pair"), ring(1))
+    mine = [own, near, back_near, far]
+    other = [lax.ppermute(w, "pair", [(0, 1), (1, 0)]) for w in mine]
 
     received = lax.all_to_all(send, "expert", split_axis=0, concat_axis=0, tiled=True)
     (back,) = call(
         ffn_kernel,
         (shape((experts, 2, HALF_CAP, blocks // 2, LANES), BF16),),
-        17,
+        9,
         scratch=[
             pltpu.VMEM((sections, slots, part), BF16),
             pltpu.VMEM((sections, experts, part), BF16),

time: 180 us -> 174 us (0.967)
  starting transfers between devices: 68 us -> 47.1 us
  waiting for transfers between devices: 84.6 us -> 99.8 us
    ppermute x14 -> x7, starting transfers between devices: 37.4 us -> 18.3 us  [the longest x4 9.06 us: one_pass(): other = [lax.ppermute(w, 'pair', [(0, 1), (1, 0)]) for w in mine]]
    all_to_all x1, waiting for transfers between devices: 0.01 us -> 16.5 us  [one_pass(): lax.all_to_all(send, 'expert', split_axis=0, concat_axis=0, tiled=True)]
    all_to_all x1, starting transfers between devices: 13.7 us -> 11.9 us  [one_pass(): lax.all_to_all(back, ('expert', 'pair'), split_axis=0, concat_axis=0, til...]
    ppermute x14 -> x7, waiting for transfers between devices: 28.6 us -> 27.3 us  [the longest x1 27.3 us: one_pass(): back_near = lax.ppermute(own, ('section', 'pair'), ring(-1))]
    unnamed x50 -> x30, local copies, waits for them, and re-layouts: 6.5 us -> 6.59 us
  transfers between devices with their start and end apart: 16 -> 9, of which waited for: 6 -> 3; matrix products, arithmetic and copies ran while one was open for 0% -> 0% of each run, Pallas kernels for 1% -> 1%
where the time goes in v3:
time: 174 us; the launch traced here: 173 us
  waiting for transfers between devices  99.8 us (57%)
  starting transfers between devices  47.1 us (27%)
  Pallas kernels  19.4 us (11%)
  local copies, waits for them, and re-layouts  6.59 us (4%)
    all_to_all x1, waiting for transfers between devices, one_pass(): lax.all_to_all(back, ('expert', 'pair'), split_axis=0, concat_axis=0, til...  56 us
    ppermute x1, waiting for transfers between devices, one_pass(): back_near = lax.ppermute(own, ('section', 'pair'), ring(-1))  27.3 us
    all_to_all x1, starting transfers between devices, one_pass(): lax.all_to_all(send, 'expert', split_axis=0, concat_axis=0, tiled=True)  16.9 us
    all_to_all x1, waiting for transfers between devices, one_pass(): lax.all_to_all(send, 'expert', split_axis=0, concat_axis=0, tiled=True)  16.5 us
    pallas_call x1, Pallas kernels, one_pass(): call(ffn_kernel, (shape((experts, 2, HALF_CAP, blocks // 2, LANES), BF16)...  12.4 us
    all_to_all x1, starting transfers between devices, one_pass(): lax.all_to_all(back, ('expert', 'pair'), split_axis=0, concat_axis=0, til...  11.9 us
    ppermute x4, starting transfers between devices, one_pass(): other = [lax.ppermute(w, 'pair', [(0, 1), (1, 0)]) for w in mine]  9.06 us
    unnamed x30, local copies, waits for them, and re-layouts  6.59 us
  transfers between devices with their start and end apart: 9, of which 3 were waited for; matrix products, arithmetic and copies ran while one was open for 0% of the time, Pallas kernels for 1%

profile of v3, /device:TPU:8, one launch (start us, length us, event | category | flops | bytes accessed | tf_op | source)
XLA Modules:
  0.0 173.1 jit_solution(9383210727256356052)
XLA Ops:
  0.0 4.1 %shard_map.91 = (bf16[64,144,128]{2,1,0:T(8,128)(2,1)}, bf16[1536,512]{1,0:T(8,128)(2,1)}) custom-call(s32[8,128]{1,0:T(8,128)} %bitcast.16, bf16[128,2048]{1,0:T(8,128)(2,1)} %state_ref.3, bf16[128,2048]{1,0:T(8,128)(2,1)} %prelude_ref.3, f32[1,2048]{1,0:T(1,128)} %bitcast.11, f32[1,2048]{1,0:T(1,128)} %bitcast.14, bf16[512,512]{1,0:T(8,128)(2,1)} %bitcast.19, ...), custom_call_target="tpu_custom_call" | custom-call | tf_op jit(solution)/shard_map/pallas_call | solution.py:299
  4.1 3.4 %collective-permute-start = (bf16[1536,512]{1,0:T(8,128)(2,1)}, bf16[1536,512]{1,0:T(8,128)(2,1)S(1)}, u32[]{:S(2)}, u32[]{:S(2)}) collective-permute-start(bf16[1536,512]{1,0:T(8,128)(2,1)} %get-tuple-element.12.refs_1_), channel_id=1, source_target_pairs={{0,128},{1,385},{128,256},{129,1},{256,384},{257,129},{384,0},{385... | collective-permute-start | bytes 4718600 | tf_op jit(solution)/shard_map/ppermute | solution.py:328
  7.5 16.9 %all-to-all-start = ((bf16[64,144,128]{2,1,0:T(8,128)(2,1)}), bf16[64,144,128]{2,1,0:T(8,128)(2,1)}, u32[]{:S(2)}, u32[]{:S(2)}) async-start(bf16[64,144,128]{2,1,0:T(8,128)(2,1)} %get-tuple-element.11), calls=%async_computation | async-start | bytes 4718592 | tf_op jit(solution)/shard_map/all_to_all | solution.py:334
  24.4 3.7 %collective-permute-start.1 = (bf16[1536,512]{1,0:T(8,128)(2,1)S(1)}, bf16[1536,512]{1,0:T(8,128)(2,1)S(1)}, u32[]{:S(2)}, u32[]{:S(2)}) collective-permute-start(bf16[1536,512]{1,0:T(8,128)(2,1)S(1)} %copy-done.10), channel_id=1, source_target_pairs={{0,384},{1,129},{128,0},{129,257},{256,128},{257,385},{384,256},{3... | collective-permute-start | bytes 4718600 | tf_op jit(solution)/shard_map/ppermute | solution.py:329
  28.1 0.0 collective-permute-done.refs_2_
  28.1 2.2 %collective-permute-start.2 = (bf16[1536,512]{1,0:T(8,128)(2,1)S(1)}, bf16[1536,512]{1,0:T(8,128)(2,1)}, u32[]{:S(2)}, u32[]{:S(2)}) collective-permute-start(bf16[1536,512]{1,0:T(8,128)(2,1)S(1)} %collective-permute-done.refs_2_), channel_id=1, source_target_pairs={{0,128},{1,385},{128,256},{129,1},{256,384},{257,129},{384,0},{385... | collective-permute-start | bytes 4718600 | tf_op jit(solution)/shard_map/ppermute | solution.py:330
  30.3 2.8 %collective-permute-start.3 = (bf16[1536,512]{1,0:T(8,128)(2,1)S(1)}, bf16[1536,512]{1,0:T(8,128)(2,1)S(1)}, u32[]{:S(2)}, u32[]{:S(2)}) collective-permute-start(bf16[1536,512]{1,0:T(8,128)(2,1)S(1)} %copy-done.10), channel_id=1, source_target_pairs={{0,1},{1,0},{2,3},{3,2},{4,5},{5,4},{6,7},{7,6},{8,9},{9,8},{10,11... | collective-permute-start | bytes 4718600 | tf_op jit(solution)/shard_map/ppermute | solution.py:332
  33.1 1.9 %collective-permute-start.4 = (bf16[1536,512]{1,0:T(8,128)(2,1)S(1)}, bf16[1536,512]{1,0:T(8,128)(2,1)S(1)}, u32[]{:S(2)}, u32[]{:S(2)}) collective-permute-start(bf16[1536,512]{1,0:T(8,128)(2,1)S(1)} %collective-permute-done.refs_2_), channel_id=1, source_target_pairs={{0,1},{1,0},{2,3},{3,2},{4,5},{5,4},{6,7},{7,6},{8,9},{9,8},{10,11... | collective-permute-start | bytes 4718600 | tf_op jit(solution)/shard_map/ppermute | solution.py:332
  35.0 27.3 %collective-permute-done.1.refs_3_ = bf16[1536,512]{1,0:T(8,128)(2,1)S(1)} collective-permute-done((bf16[1536,512]{1,0:T(8,128)(2,1)S(1)}, bf16[1536,512]{1,0:T(8,128)(2,1)S(1)}, u32[]{:S(2)}, u32[]{:S(2)}) %collective-permute-start.1) | collective-permute-done | bytes 1572896 | tf_op jit(solution)/shard_map/ppermute | solution.py:329
  62.3 1.9 %collective-permute-start.5 = (bf16[1536,512]{1,0:T(8,128)(2,1)S(1)}, bf16[1536,512]{1,0:T(8,128)(2,1)}, u32[]{:S(2)}, u32[]{:S(2)}) collective-permute-start(bf16[1536,512]{1,0:T(8,128)(2,1)S(1)} %collective-permute-done.1.refs_3_), channel_id=1, source_target_pairs={{0,1},{1,0},{2,3},{3,2},{4,5},{5,4},{6,7},{7,6},{8,9},{9,8},{10,11... | collective-permute-start | bytes 4718600 | tf_op jit(solution)/shard_map/ppermute | solution.py:332
  64.2 0.0 collective-permute-done.2.refs_4_
  64.2 2.4 %collective-permute-start.6 = (bf16[1536,512]{1,0:T(8,128)(2,1)}, bf16[1536,512]{1,0:T(8,128)(2,1)}, u32[]{:S(2)}, u32[]{:S(2)}) collective-permute-start(bf16[1536,512]{1,0:T(8,128)(2,1)} %collective-permute-done.2.refs_4_), channel_id=1, source_target_pairs={{0,1},{1,0},{2,3},{3,2},{4,5},{5,4},{6,7},{7,6},{8,9},{9,8},{10,11... | collective-permute-start | bytes 4718600 | tf_op jit(solution)/shard_map/ppermute | solution.py:332
  66.7 1.1 copy-done.13
  67.8 1.2 copy-done.14
  69.0 16.5 %all-to-all-done.refs_0_ = bf16[64,144,128]{2,1,0:T(8,128)(2,1)} async-done(((bf16[64,144,128]{2,1,0:T(8,128)(2,1)}), bf16[64,144,128]{2,1,0:T(8,128)(2,1)}, u32[]{:S(2)}, u32[]{:S(2)}) %all-to-all-start) | async-done | bytes 2359328 | tf_op jit(solution)/shard_map/all_to_all | solution.py:334
  85.5 12.4 %shard_map.92 = bf16[64,2,9,8,128]{4,3,2,1,0:T(8,128)(2,1)} custom-call(bf16[64,144,128]{2,1,0:T(8,128)(2,1)} %all-to-all-done.refs_0_, bf16[1536,512]{1,0:T(8,128)(2,1)} %get-tuple-element.12.refs_1_, bf16[1536,512]{1,0:T(8,128)(2,1)} %copy-done.11, bf16[1536,512]{1,0:T(8,128)(2,1)} %copy-done.12, bf16[1536,512]{1,0:T(8,128)(2,1)} %collective-permute-done.2.refs_4_, ...), custom_call_target="tpu_custom_call" | custom-call | tf_op jit(solution)/shard_map/pallas_call | solution.py:335
  97.9 0.0 copy-start
  97.9 0.0 copy-start.1
  97.9 0.0 copy-start.7
  98.0 0.0 copy-start.8
  98.0 0.0 copy-start.9
  98.0 11.9 %all-to-all-start.1 = ((bf16[128,72,128]{2,1,0:T(8,128)(2,1)}), bf16[128,72,128]{2,1,0:T(8,128)(2,1)S(1)}, u32[]{:S(2)}, u32[]{:S(2)}) async-start(bf16[128,72,128]{2,1,0:T(8,128)(2,1)} %bitcast.18), calls=%async_computation.1 | async-start | bytes 4718592 | tf_op jit(solution)/shard_map/all_to_all | solution.py:364
  109.9 0.0 copy-start.6
  109.9 0.9 copy-done.6
  110.9 1.2 shard_map.93
  112.1 0.0 copy-start.2
  112.1 0.7 copy-done.2
  112.8 0.7 copy-done.4
  113.5 56.0 %all-to-all-done.1.rows_ref = bf16[128,72,128]{2,1,0:T(8,128)(2,1)S(1)} async-done(((bf16[128,72,128]{2,1,0:T(8,128)(2,1)}), bf16[128,72,128]{2,1,0:T(8,128)(2,1)S(1)}, u32[]{:S(2)}, u32[]{:S(2)}) %all-to-all-start.1) | async-done | bytes 2359328 | tf_op jit(solution)/shard_map/all_to_all | solution.py:364
  169.5 0.9 copy-done.3
  170.5 0.9 copy-done.5
  171.4 1.7 shard_map.94
  (20 shorter events, 0.0 us)
Async XLA Ops:
  4.1 24.0 %collective-permute-start = (bf16[1536,512]{1,0:T(8,128)(2,1)}, bf16[1536,512]{1,0:T(8,128)(2,1)S(1)}, u32[]{:S(2)}, u32[]{:S(2)}) collective-permute-start(bf16[1536,512]{1,0:T(8,128)(2,1)} %get-tuple-element.12.refs_1_), channel_id=1, source_target_pairs={{0,128},{1,385},{128,256},{129,1},{256,384},{257,129},{384,0},{385... | collective-permute-start | bytes 4718600 | tf_op jit(solution)/shard_map/ppermute | solution.py:328
  7.5 16.9 %copy-start.10 = (bf16[1536,512]{1,0:T(8,128)(2,1)S(1)}, bf16[1536,512]{1,0:T(8,128)(2,1)}, u32[]{:S(2)}) copy-start(bf16[1536,512]{1,0:T(8,128)(2,1)} %get-tuple-element.12.refs_1_) | copy-start | bytes 4718596
  7.5 78.0 %all-to-all-start = ((bf16[64,144,128]{2,1,0:T(8,128)(2,1)}), bf16[64,144,128]{2,1,0:T(8,128)(2,1)}, u32[]{:S(2)}, u32[]{:S(2)}) async-start(bf16[64,144,128]{2,1,0:T(8,128)(2,1)} %get-tuple-element.11), calls=%async_computation | async-start | bytes 4718592 | tf_op jit(solution)/shard_map/all_to_all | solution.py:334
  24.4 37.9 %collective-permute-start.1 = (bf16[1536,512]{1,0:T(8,128)(2,1)S(1)}, bf16[1536,512]{1,0:T(8,128)(2,1)S(1)}, u32[]{:S(2)}, u32[]{:S(2)}) collective-permute-start(bf16[1536,512]{1,0:T(8,128)(2,1)S(1)} %copy-done.10), channel_id=1, source_target_pairs={{0,384},{1,129},{128,0},{129,257},{256,128},{257,385},{384,256},{3... | collective-permute-start | bytes 4718600 | tf_op jit(solution)/shard_map/ppermute | solution.py:329
  28.1 38.6 %copy-start.11 = (bf16[1536,512]{1,0:T(8,128)(2,1)}, bf16[1536,512]{1,0:T(8,128)(2,1)S(1)}, u32[]{:S(2)}) copy-start(bf16[1536,512]{1,0:T(8,128)(2,1)S(1)} %collective-permute-done.refs_2_) | copy-start | bytes 4718596
  28.1 36.2 %collective-permute-start.2 = (bf16[1536,512]{1,0:T(8,128)(2,1)S(1)}, bf16[1536,512]{1,0:T(8,128)(2,1)}, u32[]{:S(2)}, u32[]{:S(2)}) collective-permute-start(bf16[1536,512]{1,0:T(8,128)(2,1)S(1)} %collective-permute-done.refs_2_), channel_id=1, source_target_pairs={{0,128},{1,385},{128,256},{129,1},{256,384},{257,129},{384,0},{385... | collective-permute-start | bytes 4718600 | tf_op jit(solution)/shard_map/ppermute | solution.py:330
  30.3 36.4 %collective-permute-start.3 = (bf16[1536,512]{1,0:T(8,128)(2,1)S(1)}, bf16[1536,512]{1,0:T(8,128)(2,1)S(1)}, u32[]{:S(2)}, u32[]{:S(2)}) collective-permute-start(bf16[1536,512]{1,0:T(8,128)(2,1)S(1)} %copy-done.10), channel_id=1, source_target_pairs={{0,1},{1,0},{2,3},{3,2},{4,5},{5,4},{6,7},{7,6},{8,9},{9,8},{10,11... | collective-permute-start | bytes 4718600 | tf_op jit(solution)/shard_map/ppermute | solution.py:332
  33.1 33.6 %collective-permute-start.4 = (bf16[1536,512]{1,0:T(8,128)(2,1)S(1)}, bf16[1536,512]{1,0:T(8,128)(2,1)S(1)}, u32[]{:S(2)}, u32[]{:S(2)}) collective-permute-start(bf16[1536,512]{1,0:T(8,128)(2,1)S(1)} %collective-permute-done.refs_2_), channel_id=1, source_target_pairs={{0,1},{1,0},{2,3},{3,2},{4,5},{5,4},{6,7},{7,6},{8,9},{9,8},{10,11... | collective-permute-start | bytes 4718600 | tf_op jit(solution)/shard_map/ppermute | solution.py:332
  62.3 4.4 %copy-start.12 = (bf16[1536,512]{1,0:T(8,128)(2,1)}, bf16[1536,512]{1,0:T(8,128)(2,1)S(1)}, u32[]{:S(2)}) copy-start(bf16[1536,512]{1,0:T(8,128)(2,1)S(1)} %collective-permute-done.1.refs_3_) | copy-start | bytes 4718596
  62.3 6.7 %collective-permute-start.5 = (bf16[1536,512]{1,0:T(8,128)(2,1)S(1)}, bf16[1536,512]{1,0:T(8,128)(2,1)}, u32[]{:S(2)}, u32[]{:S(2)}) collective-permute-start(bf16[1536,512]{1,0:T(8,128)(2,1)S(1)} %collective-permute-done.1.refs_3_), channel_id=1, source_target_pairs={{0,1},{1,0},{2,3},{3,2},{4,5},{5,4},{6,7},{7,6},{8,9},{9,8},{10,11... | collective-permute-start | bytes 4718600 | tf_op jit(solution)/shard_map/ppermute | solution.py:332
  64.2 21.3 %collective-permute-start.6 = (bf16[1536,512]{1,0:T(8,128)(2,1)}, bf16[1536,512]{1,0:T(8,128)(2,1)}, u32[]{:S(2)}, u32[]{:S(2)}) collective-permute-start(bf16[1536,512]{1,0:T(8,128)(2,1)} %collective-permute-done.2.refs_4_), channel_id=1, source_target_pairs={{0,1},{1,0},{2,3},{3,2},{4,5},{5,4},{6,7},{7,6},{8,9},{9,8},{10,11... | collective-permute-start | bytes 4718600 | tf_op jit(solution)/shard_map/ppermute | solution.py:332
  66.7 1.2 copy-start.13
  67.8 1.2 copy-start.14
  97.9 11.9 %copy-start = (bf16[128,2048]{1,0:T(8,128)(2,1)S(1)}, bf16[128,2048]{1,0:T(8,128)(2,1)}, u32[]{:S(2)}) copy-start(bf16[128,2048]{1,0:T(8,128)(2,1)} %state_ref.3) | copy-start | bytes 1572868
  97.9 11.9 %copy-start.1 = (bf16[128,2048]{1,0:T(8,128)(2,1)S(1)}, bf16[128,2048]{1,0:T(8,128)(2,1)}, u32[]{:S(2)}) copy-start(bf16[128,2048]{1,0:T(8,128)(2,1)} %prelude_ref.3) | copy-start | bytes 1572868
  97.9 11.9 %copy-start.7 = (f32[2048]{0:T(1024)S(1)}, f32[2048]{0:T(1024)}, u32[]{:S(2)}) copy-start(f32[2048]{0:T(1024)} %param.11) | copy-start | bytes 24580
  98.0 11.9 %copy-start.8 = (f32[2048]{0:T(1024)S(1)}, f32[2048]{0:T(1024)}, u32[]{:S(2)}) copy-start(f32[2048]{0:T(1024)} %param.12) | copy-start | bytes 24580
  98.0 11.9 %copy-start.9 = (s32[1,128,8]{1,2,0:T(8,128)S(1)}, s32[1,128,8]{1,2,0:T(8,128)}, u32[]{:S(2)}) copy-start(s32[1,128,8]{1,2,0:T(8,128)} %param.17) | copy-start | bytes 12292
  98.0 71.5 %all-to-all-start.1 = ((bf16[128,72,128]{2,1,0:T(8,128)(2,1)}), bf16[128,72,128]{2,1,0:T(8,128)(2,1)S(1)}, u32[]{:S(2)}, u32[]{:S(2)}) async-start(bf16[128,72,128]{2,1,0:T(8,128)(2,1)} %bitcast.18), calls=%async_computation.1 | async-start | bytes 4718592 | tf_op jit(solution)/shard_map/all_to_all | solution.py:364
  109.9 1.0 copy-start.6
  112.1 0.7 copy-start.2
  112.8 0.7 copy-start.4
  169.5 1.0 copy-start.3
  170.5 0.9 copy-start.5

commit v4 on v3

--- a/solution.py
+++ b/solution.py
@@ -118,9 +118,9 @@
 
 def gate_kernel(
     routes_ref, state_ref, prelude_ref, inject_ref, gain_ref, router_ref,
-    main_hi_ref, main_lo_ref, last_hi_ref, last_lo_ref,
+    main_ref, last_ref,
 ):
-    experts = router_ref.shape[0]
+    tokens, experts = state_ref.shape[0], router_ref.shape[0]
     place = places(routes_ref[...], experts)
     normed = normalize(state_ref[...], prelude_ref[...], inject_ref[...], gain_ref[...])
     logits = lax.dot_general(
@@ -131,22 +131,24 @@
     gate_hi = gate.astype(BF16)
     gate_lo = (gate - gate_hi.astype(F32)).astype(BF16)
     place = place.astype(BF16)
-    for hi_ref, lo_ref, each in ((main_hi_ref, main_lo_ref, MAIN), (last_hi_ref, last_lo_ref, 1)):
+    for out_ref, each in ((main_ref, MAIN), (last_ref, 1)):
         spread = widen(experts, 2 * each)
-        lane = lax.broadcasted_iota(jnp.int32, hi_ref.shape, 1)
+        lane = lax.broadcasted_iota(jnp.int32, (tokens, out_ref.shape[1]), 1)
         core = lane // each % 2
         slot = core * HALF_CAP + (lane % each + 1 if each > 1 else HALF_CAP)
         here = dot(place, spread) == slot.astype(F32)
-        hi_ref[...] = jnp.where(here, dot(gate_hi, spread), 0.0).astype(BF16)
-        lo_ref[...] = jnp.where(here, dot(gate_lo, spread), 0.0).astype(BF16)
+        out_ref[:tokens] = jnp.where(here, dot(gate_hi, spread), 0.0).astype(BF16)
+        out_ref[tokens:] = jnp.where(here, dot(gate_lo, spread), 0.0).astype(BF16)
 
 
 def ffn_kernel(*refs):
     stored, out_ref = refs[:9], refs[9]
-    x_ref, last_ref, gate_ref, up_ref, act_ref, back_ref, ends_ref, rows_ref = refs[10:18]
-    weights, sems, row_sem, out_sems = refs[18:26], refs[26], refs[27], refs[28]
+    x_ref, last_ref, gate_ref, up_ref, act_ref, back_ref, ends_ref = refs[10:17]
+    rows_ref, first_ref, weights, sems, row_sems, out_sems = (
+        refs[17], refs[18], refs[19:27], refs[27], refs[28], refs[29],
+    )
     sections, _, part = x_ref.shape
-    experts = rows_ref.shape[0]
+    experts = rows_ref.shape[1]
     blocks = sections * part // LANES
     per = part // LANES
     main = experts * MAIN
@@ -158,7 +160,14 @@
     at = [lax.rem(here + d, sections) for d in steps]
     same = (0, 2, 1, 3)
     cut = weights[0].shape[0] // 2
-    rows_in = pltpu.make_async_copy(stored[0], rows_ref, row_sem)
+    spans = [pl.ds(pl.multiple_of(a * (per * MAIN), per * MAIN), per * MAIN) for a in at]
+    rows_in = [
+        pltpu.make_async_copy(stored[0].at[:, span, :], rows_ref.at[d], row_sems.at[d])
+        for d, span in enumerate(spans)
+    ]
+    ends_in = pltpu.make_async_copy(
+        stored[0].at[:, blocks * MAIN :, :], first_ref, row_sems.at[sections]
+    )
     copies = [
         pltpu.make_async_copy(
             stored[1 + i // 2].at[i % 2 * cut : (i % 2 + 1) * cut],
@@ -167,24 +176,31 @@
         )
         for i in range(16)
     ]
-    rows_in.start()
-    for copy in copies[:AHEAD]:
-        copy.start()
-    rows_in.wait()
-    last = rows_ref[:, blocks * MAIN :, :].astype(F32).reshape(experts, blocks * LANES)
+    ends_in.start()
+    rows_in[0].start()
+    for copy in copies[:2]:
+        copy.start()
+    for copy in rows_in[1:]:
+        copy.start()
+    for copy in copies[2:AHEAD]:
+        copy.start()
+    ends_in.wait()
+    last = first_ref[...].astype(F32).reshape(experts, blocks * LANES)
     for s in range(sections):
-        for c in range(per):
-            b = s * per + c
-            x_ref[s, :main, c * LANES : (c + 1) * LANES] = (
-                rows_ref[:, b * MAIN : (b + 1) * MAIN, :].reshape(main, LANES)
-            )
-        x_ref[s, main:, :] = last[:, s * part : (s + 1) * part].astype(BF16)
+        last_ref[s] = last[:, s * part : (s + 1) * part].astype(BF16)
 
     def piece(q, d, first, cols):
         return weights[q * 4 + d][first : first + step, cols]
 
     for q in range(2):
         for d in range(sections):
+            if q == 0:
+                rows_in[d].wait()
+                for c in range(per):
+                    x_ref[d, :main, c * LANES : (c + 1) * LANES] = (
+                        rows_ref[d, :, c * MAIN : (c + 1) * MAIN, :].reshape(main, LANES)
+                    )
+                x_ref[d, main:, :] = last_ref[at[d]]
             for i in (q * 8 + d * 2, q * 8 + d * 2 + 1):
                 copies[i].wait()
                 if i + AHEAD < len(copies):
@@ -196,7 +212,7 @@
                     total = None if d == 0 else sum_ref[:, cols]
                     for k in range(part // step):
                         term = dot(
-                            x_ref[at[d if q == 0 else same[d]], :, k * step : (k + 1) * step],
+                            x_ref[d if q == 0 else same[d], :, k * step : (k + 1) * step],
                             piece(q, d, which * part + k * step, cols),
                         )
                         total = term if total is None else total + term
@@ -249,16 +265,19 @@
         copy.wait()
 
 
-def combine_kernel(
-    rows_ref, mh_ref, ml_ref, lh_ref, ll_ref, state_ref, prelude_ref, inject_ref, out_ref
-):
-    width = out_ref.shape[1]
+def combine_kernel(rows_ref, main_ref, ends_ref, state_ref, prelude_ref, inject_ref, out_ref):
+    tokens, width = out_ref.shape
     senders = rows_ref.shape[0]
     half = width // LANES
+
+    def weigh(weights, rows):
+        both = dot(weights, rows)
+        return both[:tokens] + both[tokens:]
+
     cols = pl.ds(pl.multiple_of(lax.axis_index("pair").astype(jnp.int32) * width, width), width)
     mixed = state_ref[:, cols].astype(F32) + prelude_ref[:, cols].astype(F32) * inject_ref[:, cols]
     last = rows_ref[:, half * MAIN :, :].astype(F32).reshape(senders, width).astype(BF16)
-    mixed = mixed + (dot(lh_ref[...], last) + dot(ll_ref[...], last))
+    mixed = mixed + weigh(ends_ref[...], last)
     for pair in range(half // 2):
         rows = [
             rows_ref[:, c * MAIN : (c + 1) * MAIN, :].reshape(senders * MAIN, LANES)
@@ -266,8 +285,7 @@
         ]
         rows = jnp.concatenate(rows, axis=1)
         span = slice(pair * 2 * LANES, (pair + 1) * 2 * LANES)
-        moe = dot(mh_ref[...], rows) + dot(ml_ref[...], rows)
-        out_ref[:, span] = (mixed[:, span] + moe).astype(BF16)
+        out_ref[:, span] = (mixed[:, span] + weigh(main_ref[...], rows)).astype(BF16)
 
 
 def call(kernel, outs, n_in, scratch=(), limit=10 << 20, far=False, far_outs=0):
@@ -344,10 +362,11 @@
             pltpu.VMEM((slots, 2 * part), BF16),
             pltpu.VMEM((sections, experts, blocks // sections, MAIN, LANES), BF16),
             pltpu.VMEM((2, experts, blocks // 2, LANES), BF16),
-            pltpu.VMEM(message.shape, BF16),
+            pltpu.VMEM((sections, experts, blocks // sections * MAIN, LANES), BF16),
+            pltpu.VMEM((experts, blocks, LANES), BF16),
             *[pltpu.VMEM(w.shape, BF16) for w in mine + other],
             dma((16,)),
-            dma,
+            dma((sections + 1,)),
             dma((sections + 2,)),
         ],
         limit=WHOLE,
@@ -356,13 +375,15 @@
     )(received, *mine, *other)
     weights = call(
         gate_kernel,
-        (shape((tokens, 2 * experts * MAIN), BF16),) * 2
-        + (shape((tokens, 2 * experts), BF16),) * 2,
+        (
+            shape((2 * tokens, 2 * experts * MAIN), BF16),
+            shape((2 * tokens, 2 * experts), BF16),
+        ),
         6,
     )(*inputs, router.T)
     back = back.reshape(2 * experts, blocks // 2 * HALF_CAP, LANES)
     returned = lax.all_to_all(back, ("expert", "pair"), split_axis=0, concat_axis=0, tiled=True)
-    (out,) = call(combine_kernel, (shape((tokens, width // 2), BF16),), 8)(
+    (out,) = call(combine_kernel, (shape((tokens, width // 2), BF16),), 6)(
         returned, *weights, initial_state, prelude, inject
     )
     return out

time: 174 us -> 172 us (0.989)
    unnamed x30 -> x26, local copies, waits for them, and re-layouts: 6.59 us -> 5.15 us
where the time goes in v4:
time: 172 us; the launch traced here: 171 us
  waiting for transfers between devices  100 us (58%)
  starting transfers between devices  47.1 us (27%)
  Pallas kernels  18.7 us (11%)
  local copies, waits for them, and re-layouts  5.15 us (3%)
    all_to_all x1, waiting for transfers between devices, one_pass(): lax.all_to_all(back, ('expert', 'pair'), split_axis=0, concat_axis=0, til...  56.6 us
    ppermute x1, waiting for transfers between devices, one_pass(): back_near = lax.ppermute(own, ('section', 'pair'), ring(-1))  27.3 us
    all_to_all x1, starting transfers between devices, one_pass(): lax.all_to_all(send, 'expert', split_axis=0, concat_axis=0, tiled=True)  16.9 us
    all_to_all x1, waiting for transfers between devices, one_pass(): lax.all_to_all(send, 'expert', split_axis=0, concat_axis=0, tiled=True)  16.5 us
    all_to_all x1, starting transfers between devices, one_pass(): lax.all_to_all(back, ('expert', 'pair'), split_axis=0, concat_axis=0, til...  11.9 us
    pallas_call x1, Pallas kernels, one_pass(): call(ffn_kernel, (shape((experts, 2, HALF_CAP, blocks // 2, LANES), BF16)...  11.7 us
    ppermute x4, starting transfers between devices, one_pass(): other = [lax.ppermute(w, 'pair', [(0, 1), (1, 0)]) for w in mine]  9.06 us
    unnamed x26, local copies, waits for them, and re-layouts  5.15 us
  transfers between devices with their start and end apart: 9, of which 3 were waited for; matrix products, arithmetic and copies ran while one was open for 0% of the time, Pallas kernels for 1%

profile of v4, /device:TPU:8, one launch (start us, length us, event | category | flops | bytes accessed | tf_op | source)
XLA Modules:
  0.0 171.5 jit_solution(14414357319787513673)
XLA Ops:
  0.0 4.1 %shard_map.91 = (bf16[64,144,128]{2,1,0:T(8,128)(2,1)}, bf16[1536,512]{1,0:T(8,128)(2,1)}) custom-call(s32[8,128]{1,0:T(8,128)} %bitcast.16, bf16[128,2048]{1,0:T(8,128)(2,1)} %state_ref.3, bf16[128,2048]{1,0:T(8,128)(2,1)} %prelude_ref.3, f32[1,2048]{1,0:T(1,128)} %bitcast.11, f32[1,2048]{1,0:T(1,128)} %bitcast.14, bf16[512,512]{1,0:T(8,128)(2,1)} %bitcast.19, ...), custom_call_target="tpu_custom_call" | custom-call | tf_op jit(solution)/shard_map/pallas_call | solution.py:317
  4.1 3.4 %collective-permute-start = (bf16[1536,512]{1,0:T(8,128)(2,1)}, bf16[1536,512]{1,0:T(8,128)(2,1)S(1)}, u32[]{:S(2)}, u32[]{:S(2)}) collective-permute-start(bf16[1536,512]{1,0:T(8,128)(2,1)} %get-tuple-element.10.refs_1_), channel_id=1, source_target_pairs={{0,128},{1,385},{128,256},{129,1},{256,384},{257,129},{384,0},{385... | collective-permute-start | bytes 4718600 | tf_op jit(solution)/shard_map/ppermute | solution.py:346
  7.5 16.9 %all-to-all-start = ((bf16[64,144,128]{2,1,0:T(8,128)(2,1)}), bf16[64,144,128]{2,1,0:T(8,128)(2,1)}, u32[]{:S(2)}, u32[]{:S(2)}) async-start(bf16[64,144,128]{2,1,0:T(8,128)(2,1)} %get-tuple-element.9), calls=%async_computation | async-start | bytes 4718592 | tf_op jit(solution)/shard_map/all_to_all | solution.py:352
  24.4 3.7 %collective-permute-start.1 = (bf16[1536,512]{1,0:T(8,128)(2,1)S(1)}, bf16[1536,512]{1,0:T(8,128)(2,1)S(1)}, u32[]{:S(2)}, u32[]{:S(2)}) collective-permute-start(bf16[1536,512]{1,0:T(8,128)(2,1)S(1)} %copy-done.8), channel_id=1, source_target_pairs={{0,384},{1,129},{128,0},{129,257},{256,128},{257,385},{384,256},{3... | collective-permute-start | bytes 4718600 | tf_op jit(solution)/shard_map/ppermute | solution.py:347
  28.1 0.0 collective-permute-done.refs_2_
  28.1 2.2 %collective-permute-start.2 = (bf16[1536,512]{1,0:T(8,128)(2,1)S(1)}, bf16[1536,512]{1,0:T(8,128)(2,1)}, u32[]{:S(2)}, u32[]{:S(2)}) collective-permute-start(bf16[1536,512]{1,0:T(8,128)(2,1)S(1)} %collective-permute-done.refs_2_), channel_id=1, source_target_pairs={{0,128},{1,385},{128,256},{129,1},{256,384},{257,129},{384,0},{385... | collective-permute-start | bytes 4718600 | tf_op jit(solution)/shard_map/ppermute | solution.py:348
  30.3 2.8 %collective-permute-start.3 = (bf16[1536,512]{1,0:T(8,128)(2,1)S(1)}, bf16[1536,512]{1,0:T(8,128)(2,1)S(1)}, u32[]{:S(2)}, u32[]{:S(2)}) collective-permute-start(bf16[1536,512]{1,0:T(8,128)(2,1)S(1)} %copy-done.8), channel_id=1, source_target_pairs={{0,1},{1,0},{2,3},{3,2},{4,5},{5,4},{6,7},{7,6},{8,9},{9,8},{10,11... | collective-permute-start | bytes 4718600 | tf_op jit(solution)/shard_map/ppermute | solution.py:350
  33.1 1.9 %collective-permute-start.4 = (bf16[1536,512]{1,0:T(8,128)(2,1)S(1)}, bf16[1536,512]{1,0:T(8,128)(2,1)S(1)}, u32[]{:S(2)}, u32[]{:S(2)}) collective-permute-start(bf16[1536,512]{1,0:T(8,128)(2,1)S(1)} %collective-permute-done.refs_2_), channel_id=1, source_target_pairs={{0,1},{1,0},{2,3},{3,2},{4,5},{5,4},{6,7},{7,6},{8,9},{9,8},{10,11... | collective-permute-start | bytes 4718600 | tf_op jit(solution)/shard_map/ppermute | solution.py:350
  35.0 27.3 %collective-permute-done.1.refs_3_ = bf16[1536,512]{1,0:T(8,128)(2,1)S(1)} collective-permute-done((bf16[1536,512]{1,0:T(8,128)(2,1)S(1)}, bf16[1536,512]{1,0:T(8,128)(2,1)S(1)}, u32[]{:S(2)}, u32[]{:S(2)}) %collective-permute-start.1) | collective-permute-done | bytes 1572896 | tf_op jit(solution)/shard_map/ppermute | solution.py:347
  62.3 1.9 %collective-permute-start.5 = (bf16[1536,512]{1,0:T(8,128)(2,1)S(1)}, bf16[1536,512]{1,0:T(8,128)(2,1)}, u32[]{:S(2)}, u32[]{:S(2)}) collective-permute-start(bf16[1536,512]{1,0:T(8,128)(2,1)S(1)} %collective-permute-done.1.refs_3_), channel_id=1, source_target_pairs={{0,1},{1,0},{2,3},{3,2},{4,5},{5,4},{6,7},{7,6},{8,9},{9,8},{10,11... | collective-permute-start | bytes 4718600 | tf_op jit(solution)/shard_map/ppermute | solution.py:350
  64.2 0.0 collective-permute-done.2.refs_4_
  64.2 2.4 %collective-permute-start.6 = (bf16[1536,512]{1,0:T(8,128)(2,1)}, bf16[1536,512]{1,0:T(8,128)(2,1)}, u32[]{:S(2)}, u32[]{:S(2)}) collective-permute-start(bf16[1536,512]{1,0:T(8,128)(2,1)} %collective-permute-done.2.refs_4_), channel_id=1, source_target_pairs={{0,1},{1,0},{2,3},{3,2},{4,5},{5,4},{6,7},{7,6},{8,9},{9,8},{10,11... | collective-permute-start | bytes 4718600 | tf_op jit(solution)/shard_map/ppermute | solution.py:350
  66.7 0.0 collective-permute-done.4.refs_6_
  66.7 1.2 copy-done.11
  67.9 1.2 copy-done.12
  69.0 0.0 collective-permute-done.5.refs_7_
  69.0 16.5 %all-to-all-done.refs_0_ = bf16[64,144,128]{2,1,0:T(8,128)(2,1)} async-done(((bf16[64,144,128]{2,1,0:T(8,128)(2,1)}), bf16[64,144,128]{2,1,0:T(8,128)(2,1)}, u32[]{:S(2)}, u32[]{:S(2)}) %all-to-all-start) | async-done | bytes 2359328 | tf_op jit(solution)/shard_map/all_to_all | solution.py:352
  85.5 0.0 collective-permute-done.6.refs_8_
  85.5 11.7 %shard_map.92 = bf16[64,2,9,8,128]{4,3,2,1,0:T(8,128)(2,1)} custom-call(bf16[64,144,128]{2,1,0:T(8,128)(2,1)} %all-to-all-done.refs_0_, bf16[1536,512]{1,0:T(8,128)(2,1)} %get-tuple-element.10.refs_1_, bf16[1536,512]{1,0:T(8,128)(2,1)} %copy-done.9, bf16[1536,512]{1,0:T(8,128)(2,1)} %copy-done.10, bf16[1536,512]{1,0:T(8,128)(2,1)} %collective-permute-done.2.refs_4_, ...), custom_call_target="tpu_custom_call" | custom-call | tf_op jit(solution)/shard_map/pallas_call | solution.py:353
  97.2 0.0 copy-start
  97.2 0.0 copy-start.1
  97.3 0.0 copy-start.5
  97.3 0.0 copy-start.6
  97.3 0.0 copy-start.7
  97.3 11.9 %all-to-all-start.1 = ((bf16[128,72,128]{2,1,0:T(8,128)(2,1)}), bf16[128,72,128]{2,1,0:T(8,128)(2,1)S(1)}, u32[]{:S(2)}, u32[]{:S(2)}) async-start(bf16[128,72,128]{2,1,0:T(8,128)(2,1)} %bitcast.18), calls=%async_computation.1 | async-start | bytes 4718592 | tf_op jit(solution)/shard_map/all_to_all | solution.py:385
  109.2 0.0 copy-start.4
  109.2 0.9 copy-done.4
  110.2 1.2 shard_map.93
  111.4 0.8 copy-done.2
  112.2 56.6 %all-to-all-done.1.rows_ref = bf16[128,72,128]{2,1,0:T(8,128)(2,1)S(1)} async-done(((bf16[128,72,128]{2,1,0:T(8,128)(2,1)}), bf16[128,72,128]{2,1,0:T(8,128)(2,1)S(1)}, u32[]{:S(2)}, u32[]{:S(2)}) %all-to-all-start.1) | async-done | bytes 2359328 | tf_op jit(solution)/shard_map/all_to_all | solution.py:385
  168.8 1.0 copy-done.3
  169.9 1.6 shard_map.94
  (16 shorter events, 0.0 us)
Async XLA Ops:
  4.1 24.0 %collective-permute-start = (bf16[1536,512]{1,0:T(8,128)(2,1)}, bf16[1536,512]{1,0:T(8,128)(2,1)S(1)}, u32[]{:S(2)}, u32[]{:S(2)}) collective-permute-start(bf16[1536,512]{1,0:T(8,128)(2,1)} %get-tuple-element.10.refs_1_), channel_id=1, source_target_pairs={{0,128},{1,385},{128,256},{129,1},{256,384},{257,129},{384,0},{385... | collective-permute-start | bytes 4718600 | tf_op jit(solution)/shard_map/ppermute | solution.py:346
  7.5 16.9 %copy-start.8 = (bf16[1536,512]{1,0:T(8,128)(2,1)S(1)}, bf16[1536,512]{1,0:T(8,128)(2,1)}, u32[]{:S(2)}) copy-start(bf16[1536,512]{1,0:T(8,128)(2,1)} %get-tuple-element.10.refs_1_) | copy-start | bytes 4718596
  7.5 78.0 %all-to-all-start = ((bf16[64,144,128]{2,1,0:T(8,128)(2,1)}), bf16[64,144,128]{2,1,0:T(8,128)(2,1)}, u32[]{:S(2)}, u32[]{:S(2)}) async-start(bf16[64,144,128]{2,1,0:T(8,128)(2,1)} %get-tuple-element.9), calls=%async_computation | async-start | bytes 4718592 | tf_op jit(solution)/shard_map/all_to_all | solution.py:352
  24.4 37.9 %collective-permute-start.1 = (bf16[1536,512]{1,0:T(8,128)(2,1)S(1)}, bf16[1536,512]{1,0:T(8,128)(2,1)S(1)}, u32[]{:S(2)}, u32[]{:S(2)}) collective-permute-start(bf16[1536,512]{1,0:T(8,128)(2,1)S(1)} %copy-done.8), channel_id=1, source_target_pairs={{0,384},{1,129},{128,0},{129,257},{256,128},{257,385},{384,256},{3... | collective-permute-start | bytes 4718600 | tf_op jit(solution)/shard_map/ppermute | solution.py:347
  28.1 38.6 %copy-start.9 = (bf16[1536,512]{1,0:T(8,128)(2,1)}, bf16[1536,512]{1,0:T(8,128)(2,1)S(1)}, u32[]{:S(2)}) copy-start(bf16[1536,512]{1,0:T(8,128)(2,1)S(1)} %collective-permute-done.refs_2_) | copy-start | bytes 4718596
  28.1 36.2 %collective-permute-start.2 = (bf16[1536,512]{1,0:T(8,128)(2,1)S(1)}, bf16[1536,512]{1,0:T(8,128)(2,1)}, u32[]{:S(2)}, u32[]{:S(2)}) collective-permute-start(bf16[1536,512]{1,0:T(8,128)(2,1)S(1)} %collective-permute-done.refs_2_), channel_id=1, source_target_pairs={{0,128},{1,385},{128,256},{129,1},{256,384},{257,129},{384,0},{385... | collective-permute-start | bytes 4718600 | tf_op jit(solution)/shard_map/ppermute | solution.py:348
  30.3 36.4 %collective-permute-start.3 = (bf16[1536,512]{1,0:T(8,128)(2,1)S(1)}, bf16[1536,512]{1,0:T(8,128)(2,1)S(1)}, u32[]{:S(2)}, u32[]{:S(2)}) collective-permute-start(bf16[1536,512]{1,0:T(8,128)(2,1)S(1)} %copy-done.8), channel_id=1, source_target_pairs={{0,1},{1,0},{2,3},{3,2},{4,5},{5,4},{6,7},{7,6},{8,9},{9,8},{10,11... | collective-permute-start | bytes 4718600 | tf_op jit(solution)/shard_map/ppermute | solution.py:350
  33.1 33.6 %collective-permute-start.4 = (bf16[1536,512]{1,0:T(8,128)(2,1)S(1)}, bf16[1536,512]{1,0:T(8,128)(2,1)S(1)}, u32[]{:S(2)}, u32[]{:S(2)}) collective-permute-start(bf16[1536,512]{1,0:T(8,128)(2,1)S(1)} %collective-permute-done.refs_2_), channel_id=1, source_target_pairs={{0,1},{1,0},{2,3},{3,2},{4,5},{5,4},{6,7},{7,6},{8,9},{9,8},{10,11... | collective-permute-start | bytes 4718600 | tf_op jit(solution)/shard_map/ppermute | solution.py:350
  62.3 4.4 %copy-start.10 = (bf16[1536,512]{1,0:T(8,128)(2,1)}, bf16[1536,512]{1,0:T(8,128)(2,1)S(1)}, u32[]{:S(2)}) copy-start(bf16[1536,512]{1,0:T(8,128)(2,1)S(1)} %collective-permute-done.1.refs_3_) | copy-start | bytes 4718596
  62.3 6.7 %collective-permute-start.5 = (bf16[1536,512]{1,0:T(8,128)(2,1)S(1)}, bf16[1536,512]{1,0:T(8,128)(2,1)}, u32[]{:S(2)}, u32[]{:S(2)}) collective-permute-start(bf16[1536,512]{1,0:T(8,128)(2,1)S(1)} %collective-permute-done.1.refs_3_), channel_id=1, source_target_pairs={{0,1},{1,0},{2,3},{3,2},{4,5},{5,4},{6,7},{7,6},{8,9},{9,8},{10,11... | collective-permute-start | bytes 4718600 | tf_op jit(solution)/shard_map/ppermute | solution.py:350
  64.2 21.3 %collective-permute-start.6 = (bf16[1536,512]{1,0:T(8,128)(2,1)}, bf16[1536,512]{1,0:T(8,128)(2,1)}, u32[]{:S(2)}, u32[]{:S(2)}) collective-permute-start(bf16[1536,512]{1,0:T(8,128)(2,1)} %collective-permute-done.2.refs_4_), channel_id=1, source_target_pairs={{0,1},{1,0},{2,3},{3,2},{4,5},{5,4},{6,7},{7,6},{8,9},{9,8},{10,11... | collective-permute-start | bytes 4718600 | tf_op jit(solution)/shard_map/ppermute | solution.py:350
  66.7 1.2 copy-start.11
  67.9 1.2 copy-start.12
  97.2 11.9 %copy-start = (bf16[128,2048]{1,0:T(8,128)(2,1)S(1)}, bf16[128,2048]{1,0:T(8,128)(2,1)}, u32[]{:S(2)}) copy-start(bf16[128,2048]{1,0:T(8,128)(2,1)} %state_ref.3) | copy-start | bytes 1572868
  97.2 11.9 %copy-start.1 = (bf16[128,2048]{1,0:T(8,128)(2,1)S(1)}, bf16[128,2048]{1,0:T(8,128)(2,1)}, u32[]{:S(2)}) copy-start(bf16[128,2048]{1,0:T(8,128)(2,1)} %prelude_ref.3) | copy-start | bytes 1572868
  97.3 11.9 %copy-start.5 = (f32[2048]{0:T(1024)S(1)}, f32[2048]{0:T(1024)}, u32[]{:S(2)}) copy-start(f32[2048]{0:T(1024)} %param.11) | copy-start | bytes 24580
  97.3 11.9 %copy-start.6 = (f32[2048]{0:T(1024)S(1)}, f32[2048]{0:T(1024)}, u32[]{:S(2)}) copy-start(f32[2048]{0:T(1024)} %param.12) | copy-start | bytes 24580
  97.3 11.9 %copy-start.7 = (s32[1,128,8]{1,2,0:T(8,128)S(1)}, s32[1,128,8]{1,2,0:T(8,128)}, u32[]{:S(2)}) copy-start(s32[1,128,8]{1,2,0:T(8,128)} %param.17) | copy-start | bytes 12292
  97.3 71.5 %all-to-all-start.1 = ((bf16[128,72,128]{2,1,0:T(8,128)(2,1)}), bf16[128,72,128]{2,1,0:T(8,128)(2,1)S(1)}, u32[]{:S(2)}, u32[]{:S(2)}) async-start(bf16[128,72,128]{2,1,0:T(8,128)(2,1)} %bitcast.18), calls=%async_computation.1 | async-start | bytes 4718592 | tf_op jit(solution)/shard_map/all_to_all | solution.py:385
  109.2 1.0 copy-start.4
  111.4 0.8 copy-start.2
  168.8 1.0 copy-start.3
